TPU v7x, 768 devices: a whole 4x8x12 slice. The times are simulated.
768 devices in a mesh: row: 24 (over z_lo, x), col: 8 (over y), rep: 4 (over z_hi, core).
Axes of the slice: x: 4, y: 8, z: 12 (z_hi: 2, z_lo: 6; z = z_hi * 6 + z_lo), core: 2. Of those that a mesh axis runs over, the one named last changes fastest.
Arguments:
- vectors: float32 [8, 24576], P('rep', ('row', 'col')), may hold values from -6 to 6
- energies: float32 [24576], P(('row', 'col')), may hold values from 0 to 16
- tiles: bfloat16 [11520, 128, 128], P(('row', 'col', 'rep')), may hold values from -0.078125 to 0.078125
- tile_codes: int32 [11520], P(('row', 'col', 'rep')), may hold values from -1 to 191, as said below
Outputs:
- filtered: float32 [8, 24576], P('rep', ('row', 'col'))
- ritz_values: float32 [8], P('rep')
Inputs may be any that keep to these rules, and one draw needn't show every extreme that they name: `tile_codes`: slots of device (row, col, rep) hold tiles of grid cell (row, col) only. A code q stands for block row row * 8 + q // 24 and block column (q % 24) * 8 + col, which lies on or above the diagonal. Each cell holds its diagonal tile, each position at most once; a cell's tiles, in increasing code order, are dealt to its 4 devices in turn, so the occupied slots of a device come first and the rest are -1. Some device fills all 15 slots.
All inputs are finite; a program needn't handle non-finite values.
Results may differ from a plain program's by a relative error of at most 0.002.
Values may be sent and summed in bfloat16 or wider, within the bound.
No kernel may reach another device: no remote copies, remote signals or barrier semaphores. Data moves between devices by JAX's collectives and lax.ppermute only.
A program may use at most 32 MiB of HBM per device.

v0:
```python
import functools

import jax
import jax.numpy as jnp
from jax import lax
from jax.sharding import Mesh
from jax.sharding import PartitionSpec as P

ROW = ("row_0", "row_1")
ROW_REP = ("row_0", "row_1", "rep")
ROW_COL = ("row_0", "row_1", "col")
ROW_COL_REP = ("row_0", "row_1", "col", "rep")


filter_low = 5.0
filter_top = 20.0
spectrum_low = -3.0


def from_everyone(array, axis):
    peers = lax.axis_size(axis)
    return lax.all_to_all(
        jnp.broadcast_to(array[None], (peers, *array.shape)), axis, 0, 0, tiled=True
    )


def in_order(blocks, dim):
    blocks = jnp.moveaxis(blocks, 0, dim)
    shape = blocks.shape
    return blocks.reshape(*shape[:dim], shape[dim] * shape[dim + 1], *shape[dim + 2 :])


def gather_directly(array, axis, dim):
    blocks = from_everyone(array, axis)
    return in_order(blocks, dim)


def cut_along(array, dim, peers):
    shape = array.shape
    blocks = array.reshape(*shape[:dim], peers, shape[dim] // peers, *shape[dim + 1 :])
    return jnp.moveaxis(blocks, dim, 0)


def sent_and_summed(array, axis, dim):
    peers = lax.axis_size(axis)
    blocks = lax.all_to_all(cut_along(array, dim, peers), axis, 0, 0, tiled=True)
    return jnp.sum(blocks, axis=0)


def over_axes(array, axes):
    return functools.reduce(lax.psum, axes, array)


def on_device(vectors, energies, tiles, tile_codes):
    rows_count = lax.axis_size(ROW)
    cols_count = lax.axis_size("col")
    reps_count = lax.axis_size("rep")
    row_index = lax.axis_index(ROW)
    col_index = lax.axis_index("col")
    tile_side = tiles.shape[1]
    local_count = vectors.shape[0]
    total_count = local_count * reps_count
    present = tile_codes >= 0
    safe_code = jnp.where(present, tile_codes, 0)
    block_row = safe_code // rows_count
    block_col = safe_code % rows_count
    on_diagonal = present & (block_row == col_index) & (block_col == row_index)
    upper_mask = lax.broadcasted_iota(jnp.int32, (tile_side, tile_side), 1) > lax.broadcasted_iota(
        jnp.int32, (tile_side, tile_side), 0
    )
    keep_mask = present[:, None, None] & (
        upper_mask[None] | jnp.logical_not(on_diagonal)[:, None, None]
    )
    stored = jnp.where(keep_mask, tiles, jnp.zeros((), tiles.dtype))
    row_select = jnp.where(
        present[:, None] & (block_row[:, None] == jnp.arange(cols_count)[None, :]), 1.0, 0.0
    ).astype(jnp.float32)
    col_select = jnp.where(
        present[:, None] & (block_col[:, None] == jnp.arange(rows_count)[None, :]), 1.0, 0.0
    ).astype(jnp.float32)

    def product(vector_block):
        rounded = vector_block.astype(jnp.bfloat16)[None]
        row_group = gather_directly(rounded, ("col", "rep"), 0).reshape(
            cols_count, total_count, tile_side
        )
        col_group = lax.all_gather(rounded, ROW_REP, axis=0, tiled=True).reshape(
            rows_count, total_count, tile_side
        )
        direct = jnp.einsum(
            "svj,sij->svi", col_group[block_col], stored, preferred_element_type=jnp.float32
        )
        mirror = jnp.einsum(
            "svi,sij->svj", row_group[block_row], stored, preferred_element_type=jnp.float32
        )
        row_terms = jnp.einsum("sa,svi->avi", row_select, direct, precision=lax.Precision.HIGHEST)
        col_terms = jnp.einsum("sk,svj->kvj", col_select, mirror, precision=lax.Precision.HIGHEST)
        row_total = sent_and_summed(
            row_terms.reshape(cols_count * reps_count, local_count, tile_side), ("col", "rep"), 0
        )[0]
        partial_rows = sent_and_summed(col_terms, ROW, 0)
        col_total = sent_and_summed(partial_rows, "rep", 1)[0]
        return energies[None, :] * vector_block + row_total + col_total

    half = (filter_top - filter_low) / 2.0
    centre = (filter_top + filter_low) / 2.0
    sigma_first = half / (spectrum_low - centre)
    tau_value = 2.0 / sigma_first
    current = vectors
    previous = current
    latest = (product(current) - centre * current) * (sigma_first / half)
    sigma_next = 1.0 / (tau_value - sigma_first)
    newest = (product(latest) - centre * latest) * (
        2.0 * sigma_next / half
    ) - sigma_first * sigma_next * previous
    current = newest
    image = product(current)
    squares = over_axes(jnp.sum(current * current, axis=1), ROW_COL)
    crossed = over_axes(jnp.sum(current * image, axis=1), ROW_COL)
    ritz = crossed / (squares + 1e-06)
    resid = image - ritz[:, None] * current
    spacing = energies[None, :] - ritz[:, None]
    current = current - spacing / jnp.maximum(spacing * spacing, 1.0) * resid
    return (current, ritz)


def solution(mesh):
    split = Mesh(
        mesh.devices.reshape(6, 4, mesh.shape["col"], mesh.shape["rep"]),
        ("row_0", "row_1", "col", "rep"),
    )
    return jax.shard_map(
        on_device,
        mesh=split,
        in_specs=(P("rep", ROW_COL), P(ROW_COL), P(ROW_COL_REP, None, None), P(ROW_COL_REP)),
        out_specs=(P("rep", ROW_COL), P("rep")),
        check_vma=False,
    )
```

profile of v0, /device:TPU:8, one launch (start us, length us, event | category | flops | bytes accessed | tf_op | source)
XLA Modules:
  0.0 743.9 jit_solution(16492273548964648556)
XLA Ops:
  0.6 0.7 convert_element_type.9
  1.9 20.4 %all-to-all-start.1 = ((bf16[32,1,2,128]{3,2,1,0:T(2,128)(2,1)}), bf16[32,1,2,128]{3,2,1,0:T(2,128)(2,1)S(1)}, u32[]{:S(2)}, u32[]{:S(2)}) async-start(bf16[32,1,2,128]{3,2,1,0:T(2,128)(2,1)} %broadcast_in_dim.78), calls=%async_computation.1 | async-start | bytes 32768 | tf_op jit(solution)/shard_map/all_to_all | solution.py:22
  22.3 0.6 copy-done.1
  23.0 0.6 copy-done.2
  23.7 1.3 and_select_fusion
  25.0 158.3 %all-gather.3 = bf16[96,2,128]{2,1,0:T(2,128)(2,1)S(1)} all-gather(bf16[1,2,128]{2,1,0:T(2,128)(2,1)S(1)} %convert_bitcast_fusion), channel_id=2, replica_groups=mesh['row_0'=6,'row_1'=4,'col'=8,'rep'=4] {'row_0','row_1','rep'}, dimensions={0}, use_global_device_ids=true | all-gather | bytes 49664 | tf_op jit(solution)/shard_map/all_gather | solution.py:87
  185.7 16.0 %all-to-all-start.2 = ((f32[24,1,8,128]{3,2,1,0:T(8,128)}), f32[24,1,8,128]{3,2,1,0:T(8,128)S(1)}, u32[]{:S(2)}, u32[]{:S(2)}) async-start(f32[24,1,8,128]{3,2,1,0:T(8,128)} %copy.13), calls=%async_computation.2 | async-start | bytes 196608 | tf_op jit(solution)/shard_map/all_to_all | solution.py:46
  203.0 10.4 %all-to-all-done.2 = f32[24,1,8,128]{3,2,1,0:T(8,128)S(1)} async-done(((f32[24,1,8,128]{3,2,1,0:T(8,128)}), f32[24,1,8,128]{3,2,1,0:T(8,128)S(1)}, u32[]{:S(2)}, u32[]{:S(2)}) %all-to-all-start.2) | async-done | bytes 98336 | tf_op jit(solution)/shard_map/all_to_all | solution.py:46
  213.3 7.4 all-to-all-start
  221.3 12.9 %all-to-all-done = f32[32,1,2,128]{3,2,1,0:T(2,128)S(1)} async-done(((f32[32,1,2,128]{3,2,1,0:T(2,128)}), f32[32,1,2,128]{3,2,1,0:T(2,128)S(1)}, u32[]{:S(2)}, u32[]{:S(2)}) %all-to-all-start) | async-done | bytes 32800 | tf_op jit(solution)/shard_map/all_to_all | solution.py:46
  234.2 3.2 all-to-all-start.3
  237.5 10.0 %all-to-all-done.3 = f32[4,1,2,128]{3,2,1,0:T(2,128)S(1)} async-done(((f32[4,1,2,128]{3,2,1,0:T(2,128)}), f32[4,1,2,128]{3,2,1,0:T(2,128)S(1)}, u32[]{:S(2)}, u32[]{:S(2)}) %all-to-all-start.3) | async-done | bytes 4128 | tf_op jit(solution)/shard_map/all_to_all | solution.py:46
  248.2 4.9 all-to-all-start.5
  253.0 153.4 %all-gather.4 = bf16[96,2,128]{2,1,0:T(2,128)(2,1)S(1)} all-gather(bf16[1,2,128]{2,1,0:T(2,128)(2,1)S(1)} %bitcast.60), channel_id=3, replica_groups=mesh['row_0'=6,'row_1'=4,'col'=8,'rep'=4] {'row_0','row_1','rep'}, dimensions={0}, use_global_device_ids=true | all-gather | bytes 49664 | tf_op jit(solution)/shard_map/all_gather | solution.py:87
  408.9 18.3 %all-to-all-start.6 = ((f32[24,1,8,128]{3,2,1,0:T(8,128)}), f32[24,1,8,128]{3,2,1,0:T(8,128)S(1)}, u32[]{:S(2)}, u32[]{:S(2)}) async-start(f32[24,1,8,128]{3,2,1,0:T(8,128)} %copy.18), calls=%async_computation.6 | async-start | bytes 196608 | tf_op jit(solution)/shard_map/all_to_all | solution.py:46
  428.4 10.4 %all-to-all-done.6 = f32[24,1,8,128]{3,2,1,0:T(8,128)S(1)} async-done(((f32[24,1,8,128]{3,2,1,0:T(8,128)}), f32[24,1,8,128]{3,2,1,0:T(8,128)S(1)}, u32[]{:S(2)}, u32[]{:S(2)}) %all-to-all-start.6) | async-done | bytes 98336 | tf_op jit(solution)/shard_map/all_to_all | solution.py:46
  438.8 7.4 %all-to-all-start.4 = ((f32[32,1,2,128]{3,2,1,0:T(2,128)}), f32[32,1,2,128]{3,2,1,0:T(2,128)S(1)}, u32[]{:S(2)}, u32[]{:S(2)}) async-start(f32[32,1,2,128]{3,2,1,0:T(2,128)} %bitcast.12), calls=%async_computation.4 | async-start | bytes 65536 | tf_op jit(solution)/shard_map/all_to_all | solution.py:46
  446.8 12.9 %all-to-all-done.4 = f32[32,1,2,128]{3,2,1,0:T(2,128)S(1)} async-done(((f32[32,1,2,128]{3,2,1,0:T(2,128)}), f32[32,1,2,128]{3,2,1,0:T(2,128)S(1)}, u32[]{:S(2)}, u32[]{:S(2)}) %all-to-all-start.4) | async-done | bytes 32800 | tf_op jit(solution)/shard_map/all_to_all | solution.py:46
  459.7 3.2 all-to-all-start.7
  463.0 10.0 %all-to-all-done.7 = f32[4,1,2,128]{3,2,1,0:T(2,128)S(1)} async-done(((f32[4,1,2,128]{3,2,1,0:T(2,128)}), f32[4,1,2,128]{3,2,1,0:T(2,128)S(1)}, u32[]{:S(2)}, u32[]{:S(2)}) %all-to-all-start.7) | async-done | bytes 4128 | tf_op jit(solution)/shard_map/all_to_all | solution.py:46
  473.7 4.9 all-to-all-start.9
  478.5 153.4 %all-gather.5 = bf16[96,2,128]{2,1,0:T(2,128)(2,1)S(1)} all-gather(bf16[1,2,128]{2,1,0:T(2,128)(2,1)S(1)} %bitcast.61), channel_id=4, replica_groups=mesh['row_0'=6,'row_1'=4,'col'=8,'rep'=4] {'row_0','row_1','rep'}, dimensions={0}, use_global_device_ids=true | all-gather | bytes 49664 | tf_op jit(solution)/shard_map/all_gather | solution.py:87
  634.4 18.3 %all-to-all-start.10 = ((f32[24,1,8,128]{3,2,1,0:T(8,128)}), f32[24,1,8,128]{3,2,1,0:T(8,128)S(1)}, u32[]{:S(2)}, u32[]{:S(2)}) async-start(f32[24,1,8,128]{3,2,1,0:T(8,128)} %copy.23), calls=%async_computation.10 | async-start | bytes 196608 | tf_op jit(solution)/shard_map/all_to_all | solution.py:46
  653.9 10.4 %all-to-all-done.10 = f32[24,1,8,128]{3,2,1,0:T(8,128)S(1)} async-done(((f32[24,1,8,128]{3,2,1,0:T(8,128)}), f32[24,1,8,128]{3,2,1,0:T(8,128)S(1)}, u32[]{:S(2)}, u32[]{:S(2)}) %all-to-all-start.10) | async-done | bytes 98336 | tf_op jit(solution)/shard_map/all_to_all | solution.py:46
  664.2 7.4 %all-to-all-start.8 = ((f32[32,1,2,128]{3,2,1,0:T(2,128)}), f32[32,1,2,128]{3,2,1,0:T(2,128)S(1)}, u32[]{:S(2)}, u32[]{:S(2)}) async-start(f32[32,1,2,128]{3,2,1,0:T(2,128)} %bitcast.19), calls=%async_computation.8 | async-start | bytes 65536 | tf_op jit(solution)/shard_map/all_to_all | solution.py:46
  672.3 12.9 %all-to-all-done.8 = f32[32,1,2,128]{3,2,1,0:T(2,128)S(1)} async-done(((f32[32,1,2,128]{3,2,1,0:T(2,128)}), f32[32,1,2,128]{3,2,1,0:T(2,128)S(1)}, u32[]{:S(2)}, u32[]{:S(2)}) %all-to-all-start.8) | async-done | bytes 32800 | tf_op jit(solution)/shard_map/all_to_all | solution.py:46
  685.2 3.2 all-to-all-start.11
  688.5 10.0 %all-to-all-done.11 = f32[4,1,2,128]{3,2,1,0:T(2,128)S(1)} async-done(((f32[4,1,2,128]{3,2,1,0:T(2,128)}), f32[4,1,2,128]{3,2,1,0:T(2,128)S(1)}, u32[]{:S(2)}, u32[]{:S(2)}) %all-to-all-start.11) | async-done | bytes 4128 | tf_op jit(solution)/shard_map/all_to_all | solution.py:46
  698.7 19.8 %all-reduce.1 = (f32[2]{0:T(128)S(1)}, f32[2]{0:T(128)S(1)}) all-reduce(f32[2]{0:T(128)S(1)} %get-tuple-element.3, f32[2]{0:T(128)S(1)} %get-tuple-element.2), channel_id=1, replica_groups=mesh['row_0'=6,'row_1'=4,'col'=8,'rep'=4] {'row_0'}, use_global_device_ids=true, to_apply=%region_10.11 | all-reduce | flops 4 | bytes 32 | tf_op jit(solution)/shard_map/psum | solution.py:51
  718.5 9.3 %all-reduce.2 = (f32[2]{0:T(128)S(1)}, f32[2]{0:T(128)S(1)}) all-reduce(f32[2]{0:T(128)S(1)} %get-tuple-element.6, f32[2]{0:T(128)S(1)} %get-tuple-element.7), channel_id=1, replica_groups=mesh['row_0'=6,'row_1'=4,'col'=8,'rep'=4] {'row_1'}, use_global_device_ids=true, to_apply=%region_11.12 | all-reduce | flops 4 | bytes 32 | tf_op jit(solution)/shard_map/psum | solution.py:51
  727.8 15.5 %all-reduce = (f32[2]{0:T(128)S(1)}, f32[2]{0:T(128)S(1)}) all-reduce(f32[2]{0:T(128)S(1)} %get-tuple-element.8, f32[2]{0:T(128)S(1)} %get-tuple-element.9), channel_id=1, replica_groups=mesh['row_0'=6,'row_1'=4,'col'=8,'rep'=4] {'col'}, use_global_device_ids=true, to_apply=%region_12.13 | all-reduce | flops 4 | bytes 32 | tf_op jit(solution)/shard_map/psum | solution.py:51
  743.3 0.6 fusion.54
  (57 shorter events, 14.8 us)
Async XLA Ops:
  1.9 182.0 %all-to-all-start.1 = ((bf16[32,1,2,128]{3,2,1,0:T(2,128)(2,1)}), bf16[32,1,2,128]{3,2,1,0:T(2,128)(2,1)S(1)}, u32[]{:S(2)}, u32[]{:S(2)}) async-start(bf16[32,1,2,128]{3,2,1,0:T(2,128)(2,1)} %broadcast_in_dim.78), calls=%async_computation.1 | async-start | bytes 32768 | tf_op jit(solution)/shard_map/all_to_all | solution.py:22
  22.3 0.7 copy-start.1
  23.0 0.7 copy-start.2
  185.7 27.6 %all-to-all-start.2 = ((f32[24,1,8,128]{3,2,1,0:T(8,128)}), f32[24,1,8,128]{3,2,1,0:T(8,128)S(1)}, u32[]{:S(2)}, u32[]{:S(2)}) async-start(f32[24,1,8,128]{3,2,1,0:T(8,128)} %copy.13), calls=%async_computation.2 | async-start | bytes 196608 | tf_op jit(solution)/shard_map/all_to_all | solution.py:46
  213.3 20.9 %all-to-all-start = ((f32[32,1,2,128]{3,2,1,0:T(2,128)}), f32[32,1,2,128]{3,2,1,0:T(2,128)S(1)}, u32[]{:S(2)}, u32[]{:S(2)}) async-start(f32[32,1,2,128]{3,2,1,0:T(2,128)} %bitcast.4), calls=%async_computation | async-start | bytes 65536 | tf_op jit(solution)/shard_map/all_to_all | solution.py:46
  234.2 13.3 %all-to-all-start.3 = ((f32[4,1,2,128]{3,2,1,0:T(2,128)}), f32[4,1,2,128]{3,2,1,0:T(2,128)S(1)}, u32[]{:S(2)}, u32[]{:S(2)}) async-start(f32[4,1,2,128]{3,2,1,0:T(2,128)} %bitcast.8), calls=%async_computation.3 | async-start | bytes 8192 | tf_op jit(solution)/shard_map/all_to_all | solution.py:46
  237.5 10.0 %copy-start = (f32[128]{0:T(128)S(1)}, f32[128]{0:T(128)}, u32[]{:S(2)}) copy-start(f32[128]{0:T(128)} %param.5) | copy-start | bytes 1540
  248.2 158.9 %all-to-all-start.5 = ((bf16[32,1,2,128]{3,2,1,0:T(2,128)(2,1)}), bf16[32,1,2,128]{3,2,1,0:T(2,128)(2,1)S(1)}, u32[]{:S(2)}, u32[]{:S(2)}) async-start(bf16[32,1,2,128]{3,2,1,0:T(2,128)(2,1)} %broadcast_in_dim.81), calls=%async_computation.5 | async-start | bytes 32768 | tf_op jit(solution)/shard_map/all_to_all | solution.py:22
  408.9 29.9 %all-to-all-start.6 = ((f32[24,1,8,128]{3,2,1,0:T(8,128)}), f32[24,1,8,128]{3,2,1,0:T(8,128)S(1)}, u32[]{:S(2)}, u32[]{:S(2)}) async-start(f32[24,1,8,128]{3,2,1,0:T(8,128)} %copy.18), calls=%async_computation.6 | async-start | bytes 196608 | tf_op jit(solution)/shard_map/all_to_all | solution.py:46
  438.8 20.9 %all-to-all-start.4 = ((f32[32,1,2,128]{3,2,1,0:T(2,128)}), f32[32,1,2,128]{3,2,1,0:T(2,128)S(1)}, u32[]{:S(2)}, u32[]{:S(2)}) async-start(f32[32,1,2,128]{3,2,1,0:T(2,128)} %bitcast.12), calls=%async_computation.4 | async-start | bytes 65536 | tf_op jit(solution)/shard_map/all_to_all | solution.py:46
  459.7 13.3 %all-to-all-start.7 = ((f32[4,1,2,128]{3,2,1,0:T(2,128)}), f32[4,1,2,128]{3,2,1,0:T(2,128)S(1)}, u32[]{:S(2)}, u32[]{:S(2)}) async-start(f32[4,1,2,128]{3,2,1,0:T(2,128)} %bitcast.15), calls=%async_computation.7 | async-start | bytes 8192 | tf_op jit(solution)/shard_map/all_to_all | solution.py:46
  473.7 158.9 %all-to-all-start.9 = ((bf16[32,1,2,128]{3,2,1,0:T(2,128)(2,1)}), bf16[32,1,2,128]{3,2,1,0:T(2,128)(2,1)S(1)}, u32[]{:S(2)}, u32[]{:S(2)}) async-start(bf16[32,1,2,128]{3,2,1,0:T(2,128)(2,1)} %broadcast_in_dim.83), calls=%async_computation.9 | async-start | bytes 32768 | tf_op jit(solution)/shard_map/all_to_all | solution.py:22
  634.4 29.9 %all-to-all-start.10 = ((f32[24,1,8,128]{3,2,1,0:T(8,128)}), f32[24,1,8,128]{3,2,1,0:T(8,128)S(1)}, u32[]{:S(2)}, u32[]{:S(2)}) async-start(f32[24,1,8,128]{3,2,1,0:T(8,128)} %copy.23), calls=%async_computation.10 | async-start | bytes 196608 | tf_op jit(solution)/shard_map/all_to_all | solution.py:46
  664.2 20.9 %all-to-all-start.8 = ((f32[32,1,2,128]{3,2,1,0:T(2,128)}), f32[32,1,2,128]{3,2,1,0:T(2,128)S(1)}, u32[]{:S(2)}, u32[]{:S(2)}) async-start(f32[32,1,2,128]{3,2,1,0:T(2,128)} %bitcast.19), calls=%async_computation.8 | async-start | bytes 65536 | tf_op jit(solution)/shard_map/all_to_all | solution.py:46
  685.2 13.3 %all-to-all-start.11 = ((f32[4,1,2,128]{3,2,1,0:T(2,128)}), f32[4,1,2,128]{3,2,1,0:T(2,128)S(1)}, u32[]{:S(2)}, u32[]{:S(2)}) async-start(f32[4,1,2,128]{3,2,1,0:T(2,128)} %bitcast.22), calls=%async_computation.11 | async-start | bytes 8192 | tf_op jit(solution)/shard_map/all_to_all | solution.py:46
  743.3 0.7 copy-start.3
where the time goes:
time: 745 us; the launch traced here: 744 us
  blocking collectives  510 us (68%)
  starting transfers between devices  115 us (15%)
  waiting for transfers between devices  99.8 us (13%)
  local copies, waits for them, and re-layouts  10.3 us (1%)
    all_gather x3, blocking collectives, product(): lax.all_gather(rounded, ROW_REP, axis=0, tiled=True)  465 us
    all_to_all x9, waiting for transfers between devices, sent_and_summed(): lax.all_to_all(cut_along(array, dim, peers), axis, 0, 0, tiled=True)  99.8 us
    all_to_all x9, starting transfers between devices, sent_and_summed(): lax.all_to_all(cut_along(array, dim, peers), axis, 0, 0, tiled=True)  84.7 us
    psum x3, blocking collectives, over_axes(): return functools.reduce(lax.psum, axes, array)  44.6 us
    all_to_all x3, starting transfers between devices, from_everyone(): lax.all_to_all(jnp.broadcast_to(array[None], (peers, *array.shape)), axis...  30.1 us
  transfers between devices with their start and end apart: 12, of which 9 were waited for; matrix products, arithmetic and copies ran while one was open for 1% of the time, Pallas kernels for 0%

commit v1 on v0

v1 whole, which is shorter than its diff:
```python
import functools

import jax
import jax.numpy as jnp
from jax import lax
from jax.experimental import pallas as pl
from jax.experimental.pallas import tpu as pltpu
from jax.sharding import Mesh
from jax.sharding import PartitionSpec as P

ROW = ("z_lo", "x")
REP = ("z_hi", "core")
ROW_COL = ("z_lo", "x", "col")
ROW_COL_REP = ("z_lo", "x", "col", "z_hi", "core")

filter_low = 5.0
filter_top = 20.0
spectrum_low = -3.0

half = (filter_top - filter_low) / 2.0
centre = (filter_top + filter_low) / 2.0
sigma_first = half / (spectrum_low - centre)
tau_value = 2.0 / sigma_first
sigma_next = 1.0 / (tau_value - sigma_first)

VMEM = pl.BlockSpec(memory_space=pltpu.VMEM)
SMEM = pl.BlockSpec(memory_space=pltpu.SMEM)


def exchange(blocks, axis):
    return lax.all_to_all(blocks, axis, 0, 0, tiled=True)


def call(body, out_shapes, scalars, arrays, scratch):
    outs = [jax.ShapeDtypeStruct(shape, jnp.float32) for shape in out_shapes]
    return pl.pallas_call(
        body,
        out_shape=outs,
        in_specs=[SMEM] * len(scalars) + [VMEM] * len(arrays),
        out_specs=[VMEM] * len(outs),
        scratch_shapes=[pltpu.VMEM(shape, jnp.float32) for shape in scratch],
    )(*scalars, *arrays)


def mirror_products(table, x_ref, tile_refs, send_ref, me):
    rows, vecs = send_ref.shape[0], x_ref.shape[1]
    slots = tile_refs[0].shape[0]
    own = x_ref[me]
    for k in range(rows):
        send_ref[k, :vecs, :] = jnp.zeros_like(own)
        send_ref[k, vecs:, :] = own
    for group, tiles in enumerate(tile_refs):
        for slot in range(slots):
            a, k = table[0, group * slots + slot], table[1, group * slots + slot]
            part = lax.dot_general(
                x_ref[a].astype(jnp.bfloat16),
                tiles[slot],
                (((1,), (0,)), ((), ())),
                preferred_element_type=jnp.float32,
            )
            send_ref[k, :vecs, :] += part


def direct_products(table, got_ref, tile_refs, sums_ref):
    vecs = sums_ref.shape[1]
    slots = tile_refs[0].shape[0]
    sums_ref[...] = jnp.zeros_like(sums_ref)
    for group, tiles in enumerate(tile_refs):
        for slot in range(slots):
            a, k = table[0, group * slots + slot], table[1, group * slots + slot]
            part = lax.dot_general(
                got_ref[k, vecs:, :].astype(jnp.bfloat16),
                tiles[slot],
                (((1,), (1,)), ((), ())),
                preferred_element_type=jnp.float32,
            )
            sums_ref[a] += part


def summed_mirror(got_ref, vecs):
    total = got_ref[0, :vecs, :]
    for k in range(1, got_ref.shape[0]):
        total = total + got_ref[k, :vecs, :]
    return total


def start_kernel(table, me, first_ref, t0, t1, t2, t3, send_ref, x_ref):
    cols = first_ref.shape[0]
    vecs = x_ref.shape[1]
    for a in range(cols):
        x_ref[a] = first_ref[a, :vecs, :]
    mirror_products(table, x_ref, (t0, t1, t2, t3), send_ref, me[0])


def product_rows(got_ref, a):
    cols = got_ref.shape[0]
    total = got_ref[a, cols]
    for c in range(cols):
        total = total + got_ref[c, a]
    return total


def second_kernel(table, me, first_ref, got_ref, t0, t1, t2, t3, send_ref, x_ref):
    cols = first_ref.shape[0]
    vecs = x_ref.shape[1]
    for a in range(cols):
        x = first_ref[a, :vecs, :]
        energy = first_ref[a, vecs:, :]
        image = energy * x + product_rows(got_ref, a)
        x_ref[a] = (image - centre * x) * (sigma_first / half)
    mirror_products(table, x_ref, (t0, t1, t2, t3), send_ref, me[0])


def third_kernel(table, me, first_ref, last_ref, got_ref, t0, t1, t2, t3, send_ref, x_ref):
    cols = first_ref.shape[0]
    vecs = x_ref.shape[1]
    for a in range(cols):
        x = last_ref[a]
        energy = first_ref[a, vecs:, :]
        image = energy * x + product_rows(got_ref, a)
        x_ref[a] = (image - centre * x) * (2.0 * sigma_next / half) - (
            sigma_first * sigma_next
        ) * first_ref[a, :vecs, :]
    mirror_products(table, x_ref, (t0, t1, t2, t3), send_ref, me[0])


def direct_kernel(table, got_ref, t0, t1, t2, t3, send_ref, sums_ref):
    direct_products(table, got_ref, (t0, t1, t2, t3), sums_ref)
    cols, vecs = sums_ref.shape[0], sums_ref.shape[1]
    mirror = summed_mirror(got_ref, vecs)
    for c in range(cols):
        for a in range(cols):
            send_ref[c, a] = sums_ref[a]
        send_ref[c, cols] = mirror


def last_direct_kernel(table, me, first_ref, x_ref, got_ref, t0, t1, t2, t3, send_ref, image_ref, sums_ref):
    direct_products(table, got_ref, (t0, t1, t2, t3), sums_ref)
    cols, vecs = sums_ref.shape[0], sums_ref.shape[1]
    x = x_ref[me[0]]
    image = first_ref[me[0], vecs:, :] * x + summed_mirror(got_ref, vecs)
    image_ref[...] = image
    crossed = x * image
    for a in range(cols):
        crossed = crossed + x_ref[a] * sums_ref[a]
    for c in range(cols):
        send_ref[c, 0] = sums_ref[c]
        send_ref[c, 1] = crossed
        send_ref[c, 2] = x * x


def image_kernel(part_ref, got_ref, image_ref, send_ref):
    cols = got_ref.shape[0]
    totals = [got_ref[0, i] for i in range(3)]
    for c in range(1, cols):
        totals = [total + got_ref[c, i] for i, total in enumerate(totals)]
    image_ref[...] = part_ref[...] + totals[0]
    for k in range(send_ref.shape[0]):
        send_ref[k, 0] = totals[1]
        send_ref[k, 1] = totals[2]


def correct_kernel(me, first_ref, x_all_ref, image_ref, got_ref, out_ref, ritz_ref):
    crossed, squares = got_ref[0, 0], got_ref[0, 1]
    for k in range(1, got_ref.shape[0]):
        crossed = crossed + got_ref[k, 0]
        squares = squares + got_ref[k, 1]
    ritz = jnp.sum(crossed, axis=1, keepdims=True) / (
        jnp.sum(squares, axis=1, keepdims=True) + 1e-06
    )
    x = x_all_ref[me[0]]
    vecs = x.shape[0]
    resid = image_ref[...] - ritz * x
    spacing = first_ref[me[0], vecs:, :] - ritz
    out_ref[...] = x - spacing / jnp.maximum(spacing * spacing, 1.0) * resid
    ritz_ref[...] = jnp.broadcast_to(ritz, ritz_ref.shape)


def on_device(vectors, energies, tiles, tile_codes):
    rows = lax.axis_size(ROW)
    cols = lax.axis_size("col")
    reps = lax.axis_size(REP)
    cores = lax.axis_size("core")
    row_index = lax.axis_index(ROW)
    col_index = lax.axis_index("col")
    rep_index = lax.axis_index(REP)
    slots, side = tiles.shape[0], tiles.shape[1]
    vecs = vectors.shape[0]
    present = tile_codes >= 0
    safe_code = jnp.where(present, tile_codes, 0)
    on_diagonal = present & (safe_code == col_index * rows + row_index)
    upper_mask = lax.broadcasted_iota(jnp.int32, (side, side), 1) > lax.broadcasted_iota(
        jnp.int32, (side, side), 0
    )
    keep_mask = present[:, None, None] & (
        upper_mask[None] | jnp.logical_not(on_diagonal)[:, None, None]
    )
    stored = jnp.where(keep_mask, tiles, jnp.zeros((), tiles.dtype))
    far = lax.ppermute(stored, "z_hi", [(0, 1), (1, 0)])
    near = lax.ppermute(stored, "core", [(0, 1), (1, 0)])
    far_near = lax.ppermute(far, "core", [(0, 1), (1, 0)])
    groups = (stored, near, far, far_near)

    first = jnp.concatenate([vectors, jnp.broadcast_to(energies[None], (vecs, side))], axis=0)
    first = exchange(jnp.broadcast_to(first[None], (cols, *first.shape)), "col")
    all_codes = exchange(
        jnp.broadcast_to(safe_code[None, None], (reps, 1, slots)), REP
    ).reshape(reps, slots)
    order = rep_index ^ jnp.arange(reps, dtype=jnp.int32)
    codes = all_codes[order].reshape(reps * slots)
    table = jnp.stack([codes // rows, codes % rows])
    me = col_index.astype(jnp.int32).reshape(1)

    row_shape = (rows, 2 * vecs, side)
    state_shape = (cols, vecs, side)
    col_shape = (cols, cols + 1, vecs, side)

    def row_step(body, *arrays):
        send, x = call(body, [row_shape, state_shape], (table, me), (*arrays, *groups), [])
        return exchange(send, ROW), x

    def col_step(got):
        (send,) = call(direct_kernel, [col_shape], (table,), (got, *groups), [state_shape])
        return exchange(send, "col")

    got, _ = row_step(start_kernel, first)
    got = col_step(got)
    got, x1 = row_step(second_kernel, first, got)
    got = col_step(got)
    got, x2 = row_step(third_kernel, first, x1, got)
    send, part = call(
        last_direct_kernel,
        [(cols, 3, vecs, side), (vecs, side)],
        (table, me),
        (first, x2, got, *groups),
        [state_shape],
    )
    got = exchange(send, "col")
    image, send = call(
        image_kernel, [(vecs, side), (rows, 2, vecs, side)], (), (part, got), []
    )
    got = exchange(send, ROW)
    out, ritz = call(
        correct_kernel, [(vecs, side), (vecs, side)], (me,), (first, x2, image, got), []
    )
    return out, ritz[:, 0]


def solution(mesh):
    split = Mesh(
        mesh.devices.reshape(6, 4, mesh.shape["col"], 2, 2),
        ("z_lo", "x", "col", "z_hi", "core"),
    )
    return jax.shard_map(
        on_device,
        mesh=split,
        in_specs=(P(REP, ROW_COL), P(ROW_COL), P(ROW_COL_REP, None, None), P(ROW_COL_REP)),
        out_specs=(P(REP, ROW_COL), P(REP)),
        check_vma=False,
    )
```

time: 745 us -> 192 us (0.26)
  the two profiles are of different devices: /device:TPU:8 before, /device:TPU:2 now
where the time goes in v1:
time: 192 us; the launch traced here: 191 us
  blocking collectives  118 us (61%)
  starting transfers between devices  29.3 us (15%)
  Pallas kernels  21.2 us (11%)
  waiting for transfers between devices  13.3 us (7%)
  local copies, waits for them, and re-layouts  6.19 us (3%)
  other arithmetic  1.96 us (1%)
    all_to_all x7, blocking collectives, exchange(): return lax.all_to_all(blocks, axis, 0, 0, tiled=True)  118 us
    pallas_call x8, Pallas kernels, call(): pl.pallas_call(body, out_shape=outs, in_specs=[SMEM] * len(scalars) + [VM...  21.2 us
    ppermute x1, starting transfers between devices, on_device(): far = lax.ppermute(stored, 'z_hi', [(0, 1), (1, 0)])  15.1 us
    all_to_all x2, waiting for transfers between devices, exchange(): return lax.all_to_all(blocks, axis, 0, 0, tiled=True)  13.3 us
    all_to_all x2, starting transfers between devices, exchange(): return lax.all_to_all(blocks, axis, 0, 0, tiled=True)  10.3 us
  transfers between devices with their start and end apart: 5, of which 2 were waited for; matrix products, arithmetic and copies ran while one was open for 1% of the time, Pallas kernels for 0%

profile of v1, /device:TPU:2, one launch (start us, length us, event | category | flops | bytes accessed | tf_op | source)
XLA Modules:
  0.0 191.2 jit_solution(7556193504566362813)
XLA Ops:
  0.7 0.6 copy-done.6
  1.3 1.3 and_select_fusion.t0
  2.7 15.1 %collective-permute-start.1 = (bf16[15,128,128]{2,1,0:T(8,128)(2,1)S(1)}, bf16[15,128,128]{2,1,0:T(8,128)(2,1)S(1)}, u32[]{:S(2)}, u32[]{:S(2)}) collective-permute-start(bf16[15,128,128]{2,1,0:T(8,128)(2,1)S(1)} %and_select_fusion.t0), channel_id=1, source_target_pairs={{0,2},{2,0},{1,3},{3,1},{4,6},{6,4},{5,7},{7,5},{8,10},{10,8},{9,1... | collective-permute-start | bytes 1474568 | tf_op jit(solution)/shard_map/ppermute | solution.py:199
  17.8 1.9 %collective-permute-start = (bf16[15,128,128]{2,1,0:T(8,128)(2,1)S(1)}, bf16[15,128,128]{2,1,0:T(8,128)(2,1)S(1)}, u32[]{:S(2)}, u32[]{:S(2)}) collective-permute-start(bf16[15,128,128]{2,1,0:T(8,128)(2,1)S(1)} %and_select_fusion.t0), channel_id=1, source_target_pairs={{0,1},{1,0},{2,3},{3,2},{4,5},{5,4},{6,7},{7,6},{8,9},{9,8},{10,11... | collective-permute-start | bytes 1474568 | tf_op jit(solution)/shard_map/ppermute | solution.py:200
  19.7 0.6 broadcast_in_dim.14
  20.3 3.2 %all-to-all-start.1 = ((s32[4,1,15]{2,1,0:T(1,128)}), s32[4,1,15]{2,1,0:T(1,128)S(1)}, u32[]{:S(2)}, u32[]{:S(2)}) async-start(s32[4,1,15]{2,1,0:T(1,128)} %broadcast_in_dim.14), calls=%async_computation.1 | async-start | bytes 4096 | tf_op jit(solution)/shard_map/all_to_all | solution.py:31
  23.6 0.6 copy-done.8
  24.2 0.7 copy-done.5
  24.9 8.9 %all-to-all-done.1 = s32[4,1,15]{2,1,0:T(1,128)S(1)} async-done(((s32[4,1,15]{2,1,0:T(1,128)}), s32[4,1,15]{2,1,0:T(1,128)S(1)}, u32[]{:S(2)}, u32[]{:S(2)}) %all-to-all-start.1) | async-done | bytes 272 | tf_op jit(solution)/shard_map/all_to_all | solution.py:31
  33.8 0.6 broadcast_in_dim.13
  34.4 7.1 %all-to-all-start = ((f32[8,4,128]{2,1,0:T(4,128)}), f32[8,4,128]{2,1,0:T(4,128)S(1)}, u32[]{:S(2)}, u32[]{:S(2)}) async-start(f32[8,4,128]{2,1,0:T(4,128)} %broadcast_in_dim.13), calls=%async_computation | async-start | bytes 32768 | tf_op jit(solution)/shard_map/all_to_all | solution.py:31
  41.5 0.6 gather_fusion
  42.2 1.9 %collective-permute-start.2 = (bf16[15,128,128]{2,1,0:T(8,128)(2,1)S(1)}, bf16[15,128,128]{2,1,0:T(8,128)(2,1)S(1)}, u32[]{:S(2)}, u32[]{:S(2)}) collective-permute-start(bf16[15,128,128]{2,1,0:T(8,128)(2,1)S(1)} %collective-permute-done.1.t2), channel_id=1, source_target_pairs={{0,1},{1,0},{2,3},{3,2},{4,5},{5,4},{6,7},{7,6},{8,9},{9,8},{10,11... | collective-permute-start | bytes 1474568 | tf_op jit(solution)/shard_map/ppermute | solution.py:201
  44.3 0.6 pad_add_fusion.table
  44.8 4.4 %all-to-all-done.first_ref = f32[8,4,128]{2,1,0:T(4,128)S(1)} async-done(((f32[8,4,128]{2,1,0:T(4,128)}), f32[8,4,128]{2,1,0:T(4,128)S(1)}, u32[]{:S(2)}, u32[]{:S(2)}) %all-to-all-start) | async-done | bytes 16416 | tf_op jit(solution)/shard_map/all_to_all | solution.py:31
  50.2 2.8 %shard_map.59 = (f32[24,4,128]{2,1,0:T(4,128)}, f32[8,2,128]{2,1,0:T(2,128)}) custom-call(s32[2,60]{1,0:T(2,128)} %pad_add_fusion.table, s32[1]{0:T(128)} %bitcast.me, f32[8,4,128]{2,1,0:T(4,128)} %copy-done.4, bf16[15,128,128]{2,1,0:T(8,128)(2,1)} %copy-done, bf16[15,128,128]{2,1,0:T(8,128)(2,1)} %copy-done.2, bf16[15,128,128]{2,1,0:T(8,128)(2,1)} %copy-done.1, ...), custom_call_target="tpu_custom_call" | custom-call | tf_op jit(solution)/shard_map/pallas_call | solution.py:36
  53.0 35.5 %all_to_all.45.got_ref = f32[24,4,128]{2,1,0:T(4,128)} all-to-all(f32[24,4,128]{2,1,0:T(4,128)} %get-tuple-element.13), channel_id=1, replica_groups=mesh['z_lo'=6,'x'=4,'col'=8,'z_hi'=2,'core'=2] {'z_lo','x'}, dimensions={0} | all-to-all | bytes 98304 | tf_op jit(solution)/shard_map/all_to_all | solution.py:31
  88.5 3.3 %shard_map.60 = f32[8,9,2,128]{3,2,1,0:T(2,128)} custom-call(s32[2,60]{1,0:T(2,128)} %pad_add_fusion.table, f32[24,4,128]{2,1,0:T(4,128)} %all_to_all.45.got_ref, bf16[15,128,128]{2,1,0:T(8,128)(2,1)} %copy-done, bf16[15,128,128]{2,1,0:T(8,128)(2,1)} %copy-done.2, bf16[15,128,128]{2,1,0:T(8,128)(2,1)} %copy-done.1, bf16[15,128,128]{2,1,0:T(8,128)(2,1)} %copy-done.3), custom_call_target="tpu_custom_call" | custom-call | tf_op jit(solution)/shard_map/pallas_call | solution.py:36
  91.8 12.4 %all_to_all.46.got_ref = f32[8,9,2,128]{3,2,1,0:T(2,128)} all-to-all(f32[8,9,2,128]{3,2,1,0:T(2,128)} %shard_map.60), channel_id=1, replica_groups=mesh['z_lo'=6,'x'=4,'col'=8,'z_hi'=2,'core'=2] {'col'}, dimensions={0} | all-to-all | bytes 147456 | tf_op jit(solution)/shard_map/all_to_all | solution.py:31
  104.2 2.8 %shard_map.61 = (f32[24,4,128]{2,1,0:T(4,128)}, f32[8,2,128]{2,1,0:T(2,128)}) custom-call(s32[2,60]{1,0:T(2,128)} %pad_add_fusion.table, s32[1]{0:T(128)} %bitcast.me, f32[8,4,128]{2,1,0:T(4,128)} %copy-done.4, f32[8,9,2,128]{3,2,1,0:T(2,128)} %all_to_all.46.got_ref, bf16[15,128,128]{2,1,0:T(8,128)(2,1)} %copy-done, bf16[15,128,128]{2,1,0:T(8,128)(2,1)} %copy-done.2, ...), custom_call_target="tpu_custom_call" | custom-call | tf_op jit(solution)/shard_map/pallas_call | solution.py:36
  107.0 15.4 %all_to_all.47.got_ref = f32[24,4,128]{2,1,0:T(4,128)} all-to-all(f32[24,4,128]{2,1,0:T(4,128)} %get-tuple-element.15), channel_id=1, replica_groups=mesh['z_lo'=6,'x'=4,'col'=8,'z_hi'=2,'core'=2] {'z_lo','x'}, dimensions={0} | all-to-all | bytes 98304 | tf_op jit(solution)/shard_map/all_to_all | solution.py:31
  122.4 3.3 %shard_map.62 = f32[8,9,2,128]{3,2,1,0:T(2,128)} custom-call(s32[2,60]{1,0:T(2,128)} %pad_add_fusion.table, f32[24,4,128]{2,1,0:T(4,128)} %all_to_all.47.got_ref, bf16[15,128,128]{2,1,0:T(8,128)(2,1)} %copy-done, bf16[15,128,128]{2,1,0:T(8,128)(2,1)} %copy-done.2, bf16[15,128,128]{2,1,0:T(8,128)(2,1)} %copy-done.1, bf16[15,128,128]{2,1,0:T(8,128)(2,1)} %copy-done.3), custom_call_target="tpu_custom_call" | custom-call | tf_op jit(solution)/shard_map/pallas_call | solution.py:36
  125.7 12.4 %all_to_all.48.got_ref = f32[8,9,2,128]{3,2,1,0:T(2,128)} all-to-all(f32[8,9,2,128]{3,2,1,0:T(2,128)} %shard_map.62), channel_id=1, replica_groups=mesh['z_lo'=6,'x'=4,'col'=8,'z_hi'=2,'core'=2] {'col'}, dimensions={0} | all-to-all | bytes 147456 | tf_op jit(solution)/shard_map/all_to_all | solution.py:31
  138.2 2.8 %shard_map.63 = (f32[24,4,128]{2,1,0:T(4,128)}, f32[8,2,128]{2,1,0:T(2,128)}) custom-call(s32[2,60]{1,0:T(2,128)} %pad_add_fusion.table, s32[1]{0:T(128)} %bitcast.me, f32[8,4,128]{2,1,0:T(4,128)} %copy-done.4, f32[8,2,128]{2,1,0:T(2,128)} %get-tuple-element.14.last_ref, f32[8,9,2,128]{3,2,1,0:T(2,128)} %all_to_all.48.got_ref, ...), custom_call_target="tpu_custom_call" | custom-call | tf_op jit(solution)/shard_map/pallas_call | solution.py:36
  141.0 15.4 %all_to_all.49.got_ref = f32[24,4,128]{2,1,0:T(4,128)} all-to-all(f32[24,4,128]{2,1,0:T(4,128)} %get-tuple-element.17), channel_id=1, replica_groups=mesh['z_lo'=6,'x'=4,'col'=8,'z_hi'=2,'core'=2] {'z_lo','x'}, dimensions={0} | all-to-all | bytes 98304 | tf_op jit(solution)/shard_map/all_to_all | solution.py:31
  156.4 3.3 %shard_map.64 = (f32[8,3,2,128]{3,2,1,0:T(2,128)}, f32[2,128]{1,0:T(2,128)}) custom-call(s32[2,60]{1,0:T(2,128)} %pad_add_fusion.table, s32[1]{0:T(128)} %bitcast.me, f32[8,4,128]{2,1,0:T(4,128)} %copy-done.4, f32[8,2,128]{2,1,0:T(2,128)} %get-tuple-element.16.x_ref.x_all_ref, f32[24,4,128]{2,1,0:T(4,128)} %all_to_all.49.got_ref, ...), custom_call_target="tpu_custom_call" | custom-call | tf_op jit(solution)/shard_map/pallas_call | solution.py:36
  159.7 11.9 %all_to_all.50.got_ref = f32[8,3,2,128]{3,2,1,0:T(2,128)} all-to-all(f32[8,3,2,128]{3,2,1,0:T(2,128)} %get-tuple-element.19), channel_id=1, replica_groups=mesh['z_lo'=6,'x'=4,'col'=8,'z_hi'=2,'core'=2] {'col'}, dimensions={0} | all-to-all | bytes 49152 | tf_op jit(solution)/shard_map/all_to_all | solution.py:31
  171.6 1.4 shard_map.65
  173.0 15.4 %all_to_all.51.got_ref = f32[24,2,2,128]{3,2,1,0:T(2,128)} all-to-all(f32[24,2,2,128]{3,2,1,0:T(2,128)} %get-tuple-element.21), channel_id=1, replica_groups=mesh['z_lo'=6,'x'=4,'col'=8,'z_hi'=2,'core'=2] {'z_lo','x'}, dimensions={0} | all-to-all | bytes 98304 | tf_op jit(solution)/shard_map/all_to_all | solution.py:31
  188.4 1.5 shard_map.66
  189.9 0.7 copy-done.7
  190.6 0.6 slice_reduce_fusion
  (30 shorter events, 1.3 us)
Async XLA Ops:
  0.7 0.7 copy-start.6
  2.7 46.6 %copy-start = (bf16[15,128,128]{2,1,0:T(8,128)(2,1)}, bf16[15,128,128]{2,1,0:T(8,128)(2,1)S(1)}, u32[]{:S(2)}) copy-start(bf16[15,128,128]{2,1,0:T(8,128)(2,1)S(1)} %and_select_fusion.t0) | copy-start | bytes 1474564
  2.7 39.5 %collective-permute-start.1 = (bf16[15,128,128]{2,1,0:T(8,128)(2,1)S(1)}, bf16[15,128,128]{2,1,0:T(8,128)(2,1)S(1)}, u32[]{:S(2)}, u32[]{:S(2)}) collective-permute-start(bf16[15,128,128]{2,1,0:T(8,128)(2,1)S(1)} %and_select_fusion.t0), channel_id=1, source_target_pairs={{0,2},{2,0},{1,3},{3,1},{4,6},{6,4},{5,7},{7,5},{8,10},{10,8},{9,1... | collective-permute-start | bytes 1474568 | tf_op jit(solution)/shard_map/ppermute | solution.py:199
  17.8 31.5 %collective-permute-start = (bf16[15,128,128]{2,1,0:T(8,128)(2,1)S(1)}, bf16[15,128,128]{2,1,0:T(8,128)(2,1)S(1)}, u32[]{:S(2)}, u32[]{:S(2)}) collective-permute-start(bf16[15,128,128]{2,1,0:T(8,128)(2,1)S(1)} %and_select_fusion.t0), channel_id=1, source_target_pairs={{0,1},{1,0},{2,3},{3,2},{4,5},{5,4},{6,7},{7,6},{8,9},{9,8},{10,11... | collective-permute-start | bytes 1474568 | tf_op jit(solution)/shard_map/ppermute | solution.py:200
  20.3 13.5 %all-to-all-start.1 = ((s32[4,1,15]{2,1,0:T(1,128)}), s32[4,1,15]{2,1,0:T(1,128)S(1)}, u32[]{:S(2)}, u32[]{:S(2)}) async-start(s32[4,1,15]{2,1,0:T(1,128)} %broadcast_in_dim.14), calls=%async_computation.1 | async-start | bytes 4096 | tf_op jit(solution)/shard_map/all_to_all | solution.py:31
  23.6 0.7 copy-start.8
  24.2 0.7 copy-start.5
  34.4 14.9 %all-to-all-start = ((f32[8,4,128]{2,1,0:T(4,128)}), f32[8,4,128]{2,1,0:T(4,128)S(1)}, u32[]{:S(2)}, u32[]{:S(2)}) async-start(f32[8,4,128]{2,1,0:T(4,128)} %broadcast_in_dim.13), calls=%async_computation | async-start | bytes 32768 | tf_op jit(solution)/shard_map/all_to_all | solution.py:31
  42.2 7.2 %copy-start.1 = (bf16[15,128,128]{2,1,0:T(8,128)(2,1)}, bf16[15,128,128]{2,1,0:T(8,128)(2,1)S(1)}, u32[]{:S(2)}) copy-start(bf16[15,128,128]{2,1,0:T(8,128)(2,1)S(1)} %collective-permute-done.1.t2) | copy-start | bytes 1474564
  42.2 7.1 %collective-permute-start.2 = (bf16[15,128,128]{2,1,0:T(8,128)(2,1)S(1)}, bf16[15,128,128]{2,1,0:T(8,128)(2,1)S(1)}, u32[]{:S(2)}, u32[]{:S(2)}) collective-permute-start(bf16[15,128,128]{2,1,0:T(8,128)(2,1)S(1)} %collective-permute-done.1.t2), channel_id=1, source_target_pairs={{0,1},{1,0},{2,3},{3,2},{4,5},{5,4},{6,7},{7,6},{8,9},{9,8},{10,11... | collective-permute-start | bytes 1474568 | tf_op jit(solution)/shard_map/ppermute | solution.py:201
  49.3 0.6 copy-start.4
  49.3 0.8 copy-start.2
  49.3 1.0 copy-start.3
  189.9 0.7 copy-start.7

commit v2 on v1

--- a/solution.py
+++ b/solution.py
@@ -1,5 +1,3 @@
-import functools
-
 import jax
 import jax.numpy as jnp
 from jax import lax
@@ -42,16 +40,22 @@
     )(*scalars, *arrays)
 
 
+def place(code, rows):
+    shift = 16
+    a = (code * (-(-(1 << shift) // rows))) >> shift
+    return a, code - a * rows
+
+
 def mirror_products(table, x_ref, tile_refs, send_ref, me):
     rows, vecs = send_ref.shape[0], x_ref.shape[1]
-    slots = tile_refs[0].shape[0]
+    slots = tile_refs[0].shape[0] - 1
     own = x_ref[me]
     for k in range(rows):
         send_ref[k, :vecs, :] = jnp.zeros_like(own)
         send_ref[k, vecs:, :] = own
     for group, tiles in enumerate(tile_refs):
         for slot in range(slots):
-            a, k = table[0, group * slots + slot], table[1, group * slots + slot]
+            a, k = place(table[group * slots + slot], rows)
             part = lax.dot_general(
                 x_ref[a].astype(jnp.bfloat16),
                 tiles[slot],
@@ -63,11 +67,12 @@
 
 def direct_products(table, got_ref, tile_refs, sums_ref):
     vecs = sums_ref.shape[1]
-    slots = tile_refs[0].shape[0]
+    rows = got_ref.shape[0]
+    slots = tile_refs[0].shape[0] - 1
     sums_ref[...] = jnp.zeros_like(sums_ref)
     for group, tiles in enumerate(tile_refs):
         for slot in range(slots):
-            a, k = table[0, group * slots + slot], table[1, group * slots + slot]
+            a, k = place(table[group * slots + slot], rows)
             part = lax.dot_general(
                 got_ref[k, vecs:, :].astype(jnp.bfloat16),
                 tiles[slot],
@@ -84,18 +89,23 @@
     return total
 
 
-def start_kernel(table, me, first_ref, t0, t1, t2, t3, send_ref, x_ref):
-    cols = first_ref.shape[0]
-    vecs = x_ref.shape[1]
-    for a in range(cols):
-        x_ref[a] = first_ref[a, :vecs, :]
-    mirror_products(table, x_ref, (t0, t1, t2, t3), send_ref, me[0])
+def start_kernel(table, me, first_ref, t0, t1, send_ref, base_ref, x_ref):
+    cols, vecs = base_ref.shape[0], base_ref.shape[1] // 2
+    halves = first_ref.shape[0] // cols
+    for a in range(cols):
+        for z in range(halves):
+            x_ref[a, z * vecs : (z + 1) * vecs, :] = first_ref[a * halves + z, :vecs, :]
+        base_ref[a] = first_ref[a * halves + me[1]]
+    mirror_products(table, x_ref, (t0, t1), send_ref, me[0])
 
 
 def product_rows(got_ref, a):
-    cols = got_ref.shape[0]
-    total = got_ref[a, cols]
-    for c in range(cols):
+    peers, cols = got_ref.shape[0], got_ref.shape[1] - 1
+    halves = peers // cols
+    total = got_ref[a * halves, cols]
+    for z in range(1, halves):
+        total = total + got_ref[a * halves + z, cols]
+    for c in range(peers):
         total = total + got_ref[c, a]
     return total
 
@@ -124,14 +134,18 @@
     mirror_products(table, x_ref, (t0, t1, t2, t3), send_ref, me[0])
 
 
-def direct_kernel(table, got_ref, t0, t1, t2, t3, send_ref, sums_ref):
-    direct_products(table, got_ref, (t0, t1, t2, t3), sums_ref)
-    cols, vecs = sums_ref.shape[0], sums_ref.shape[1]
-    mirror = summed_mirror(got_ref, vecs)
-    for c in range(cols):
-        for a in range(cols):
-            send_ref[c, a] = sums_ref[a]
-        send_ref[c, cols] = mirror
+def direct_kernel(table, got_ref, *refs):
+    *tiles, send_ref, sums_ref = refs
+    direct_products(table, got_ref, tiles, sums_ref)
+    cols, vecs = sums_ref.shape[0], send_ref.shape[2]
+    halves = send_ref.shape[0] // cols
+    mirror = summed_mirror(got_ref, vecs * halves)
+    for z in range(halves):
+        part = slice(z * vecs, (z + 1) * vecs)
+        for c in range(cols):
+            for a in range(cols):
+                send_ref[c * halves + z, a] = sums_ref[a, part, :]
+            send_ref[c * halves + z, cols] = mirror[part]
 
 
 def last_direct_kernel(table, me, first_ref, x_ref, got_ref, t0, t1, t2, t3, send_ref, image_ref, sums_ref):
@@ -179,11 +193,10 @@
 def on_device(vectors, energies, tiles, tile_codes):
     rows = lax.axis_size(ROW)
     cols = lax.axis_size("col")
-    reps = lax.axis_size(REP)
-    cores = lax.axis_size("core")
+    halves = lax.axis_size("z_hi")
     row_index = lax.axis_index(ROW)
     col_index = lax.axis_index("col")
-    rep_index = lax.axis_index(REP)
+    half_index = lax.axis_index("z_hi")
     slots, side = tiles.shape[0], tiles.shape[1]
     vecs = vectors.shape[0]
     present = tile_codes >= 0
@@ -196,43 +209,60 @@
         upper_mask[None] | jnp.logical_not(on_diagonal)[:, None, None]
     )
     stored = jnp.where(keep_mask, tiles, jnp.zeros((), tiles.dtype))
-    far = lax.ppermute(stored, "z_hi", [(0, 1), (1, 0)])
-    near = lax.ppermute(stored, "core", [(0, 1), (1, 0)])
-    far_near = lax.ppermute(far, "core", [(0, 1), (1, 0)])
-    groups = (stored, near, far, far_near)
+    label = jnp.broadcast_to(
+        jnp.pad(safe_code.astype(tiles.dtype), (0, side - slots))[None, None], (1, side, side)
+    )
+    stored = jnp.concatenate([stored, label], axis=0)
+    swap = [(0, 1), (1, 0)]
+    far = lax.ppermute(stored, "z_hi", swap)
+    near = lax.ppermute(stored, "core", swap)
+
+    def codes_of(group):
+        return group[slots, 0, :slots].astype(jnp.int32)
 
     first = jnp.concatenate([vectors, jnp.broadcast_to(energies[None], (vecs, side))], axis=0)
-    first = exchange(jnp.broadcast_to(first[None], (cols, *first.shape)), "col")
-    all_codes = exchange(
-        jnp.broadcast_to(safe_code[None, None], (reps, 1, slots)), REP
-    ).reshape(reps, slots)
-    order = rep_index ^ jnp.arange(reps, dtype=jnp.int32)
-    codes = all_codes[order].reshape(reps * slots)
-    table = jnp.stack([codes // rows, codes % rows])
-    me = col_index.astype(jnp.int32).reshape(1)
-
-    row_shape = (rows, 2 * vecs, side)
+    first = jnp.broadcast_to(first[None], (cols * halves, *first.shape))
+    first = exchange(first, ("col", "z_hi"))
+    me = jnp.stack([col_index, half_index]).astype(jnp.int32)
+
     state_shape = (cols, vecs, side)
     col_shape = (cols, cols + 1, vecs, side)
+    pair_shape = (cols * halves, cols + 1, vecs, side)
+
+    pair = (stored, near)
+    pair_codes = jnp.concatenate([safe_code, codes_of(near)])
+    send, base = call(
+        start_kernel,
+        [(rows, 2 * halves * vecs, side), (cols, 2 * vecs, side)],
+        (pair_codes, me),
+        (first, *pair),
+        [(cols, halves * vecs, side)],
+    )
+    got = exchange(send, ROW)
+    (send,) = call(
+        direct_kernel, [pair_shape], (pair_codes,), (got, *pair), [(cols, halves * vecs, side)]
+    )
+    far, _ = lax.optimization_barrier((far, send))
+    got = exchange(send, ("col", "z_hi"))
+    far_near = lax.ppermute(far, "core", swap)
+    groups = (stored, near, far, far_near)
+    codes = jnp.concatenate([pair_codes, codes_of(far), codes_of(far_near)])
 
     def row_step(body, *arrays):
-        send, x = call(body, [row_shape, state_shape], (table, me), (*arrays, *groups), [])
+        send, x = call(
+            body, [(rows, 2 * vecs, side), state_shape], (codes, me), (*arrays, *groups), []
+        )
         return exchange(send, ROW), x
 
-    def col_step(got):
-        (send,) = call(direct_kernel, [col_shape], (table,), (got, *groups), [state_shape])
-        return exchange(send, "col")
-
-    got, _ = row_step(start_kernel, first)
-    got = col_step(got)
-    got, x1 = row_step(second_kernel, first, got)
-    got = col_step(got)
-    got, x2 = row_step(third_kernel, first, x1, got)
+    got, x1 = row_step(second_kernel, base, got)
+    (send,) = call(direct_kernel, [col_shape], (codes,), (got, *groups), [state_shape])
+    got = exchange(send, "col")
+    got, x2 = row_step(third_kernel, base, x1, got)
     send, part = call(
         last_direct_kernel,
         [(cols, 3, vecs, side), (vecs, side)],
-        (table, me),
-        (first, x2, got, *groups),
+        (codes, me),
+        (base, x2, got, *groups),
         [state_shape],
     )
     got = exchange(send, "col")
@@ -241,7 +271,7 @@
     )
     got = exchange(send, ROW)
     out, ritz = call(
-        correct_kernel, [(vecs, side), (vecs, side)], (me,), (first, x2, image, got), []
+        correct_kernel, [(vecs, side), (vecs, side)], (me,), (base, x2, image, got), []
     )
     return out, ritz[:, 0]
 

time: 192 us -> 203 us (1.057)
  waiting for transfers between devices: 13.3 us -> 28.6 us
  blocking collectives: 118 us -> 109 us
  starting transfers between devices: 29.3 us -> 35.9 us
  local copies, waits for them, and re-layouts: 6.19 us -> 3.86 us
    all_to_all x2, waiting for transfers between devices: 13.3 us -> 28.6 us  [exchange(): return lax.all_to_all(blocks, axis, 0, 0, tiled=True)]
    all_to_all x7 -> x6, blocking collectives: 118 us -> 109 us  [exchange(): return lax.all_to_all(blocks, axis, 0, 0, tiled=True)]
    all_to_all x2, starting transfers between devices: 10.3 us -> 16.8 us  [exchange(): return lax.all_to_all(blocks, axis, 0, 0, tiled=True)]
  transfers between devices with their start and end apart: 5 -> 5, of which waited for: 2 -> 2; matrix products, arithmetic and copies ran while one was open for 1% -> 1% of each run, Pallas kernels for 0% -> 2%
where the time goes in v2:
time: 203 us; the launch traced here: 202 us
  blocking collectives  109 us (54%)
  starting transfers between devices  35.9 us (18%)
  waiting for transfers between devices  28.6 us (14%)
  Pallas kernels  20.3 us (10%)
  local copies, waits for them, and re-layouts  3.86 us (2%)
  other arithmetic  3.42 us (2%)
    all_to_all x6, blocking collectives, exchange(): return lax.all_to_all(blocks, axis, 0, 0, tiled=True)  109 us
    all_to_all x2, waiting for transfers between devices, exchange(): return lax.all_to_all(blocks, axis, 0, 0, tiled=True)  28.6 us
    pallas_call x8, Pallas kernels, call(): pl.pallas_call(body, out_shape=outs, in_specs=[SMEM] * len(scalars) + [VM...  20.3 us
    all_to_all x2, starting transfers between devices, exchange(): return lax.all_to_all(blocks, axis, 0, 0, tiled=True)  16.8 us
    ppermute x1, starting transfers between devices, on_device(): far = lax.ppermute(stored, 'z_hi', swap)  15.1 us
  transfers between devices with their start and end apart: 5, of which 2 were waited for; matrix products, arithmetic and copies ran while one was open for 1% of the time, Pallas kernels for 2%

profile of v2, /device:TPU:2, one launch (start us, length us, event | category | flops | bytes accessed | tf_op | source)
XLA Modules:
  0.0 201.9 jit_solution(5823725592388830349)
XLA Ops:
  0.7 0.0 copy-start.7
  0.7 0.6 copy-done.7
  1.4 1.3 and_select_fusion
  2.8 2.1 %collective-permute-start = (bf16[16,128,128]{2,1,0:T(8,128)(2,1)S(1)}, bf16[16,128,128]{2,1,0:T(8,128)(2,1)S(1)}, u32[]{:S(2)}, u32[]{:S(2)}) collective-permute-start(bf16[16,128,128]{2,1,0:T(8,128)(2,1)S(1)} %pad_maximum_fusion.t0.refs_0_), channel_id=1, source_target_pairs={{0,1},{1,0},{2,3},{3,2},{4,5},{5,4},{6,7},{7,6},{8,9},{9,8},{10,11... | collective-permute-start | bytes 1572872 | tf_op jit(solution)/shard_map/ppermute | solution.py:218
  4.8 15.1 %collective-permute-start.1 = (bf16[16,128,128]{2,1,0:T(8,128)(2,1)S(1)}, bf16[16,128,128]{2,1,0:T(8,128)(2,1)S(1)}, u32[]{:S(2)}, u32[]{:S(2)}) collective-permute-start(bf16[16,128,128]{2,1,0:T(8,128)(2,1)S(1)} %pad_maximum_fusion.t0.refs_0_), channel_id=1, source_target_pairs={{0,2},{2,0},{1,3},{3,1},{4,6},{6,4},{5,7},{7,5},{8,10},{10,8},{9,1... | collective-permute-start | bytes 1572872 | tf_op jit(solution)/shard_map/ppermute | solution.py:217
  20.0 0.6 broadcast_in_dim.15
  20.6 7.2 %all-to-all-start = ((f32[16,4,128]{2,1,0:T(4,128)}), f32[16,4,128]{2,1,0:T(4,128)S(1)}, u32[]{:S(2)}, u32[]{:S(2)}) async-start(f32[16,4,128]{2,1,0:T(4,128)} %broadcast_in_dim.15), calls=%async_computation | async-start | bytes 65536 | tf_op jit(solution)/shard_map/all_to_all | solution.py:29
  27.9 0.7 pad_add_fusion.me
  28.5 0.7 pad_add_fusion.1.table
  29.2 13.8 %all-to-all-done.first_ref = f32[16,4,128]{2,1,0:T(4,128)S(1)} async-done(((f32[16,4,128]{2,1,0:T(4,128)}), f32[16,4,128]{2,1,0:T(4,128)S(1)}, u32[]{:S(2)}, u32[]{:S(2)}) %all-to-all-start) | async-done | bytes 32800 | tf_op jit(solution)/shard_map/all_to_all | solution.py:29
  43.0 0.6 copy-done.5
  43.6 2.2 %shard_map.59 = (f32[24,8,128]{2,1,0:T(8,128)}, f32[8,4,128]{2,1,0:T(4,128)}) custom-call(s32[30]{0:T(128)} %pad_add_fusion.1.table, s32[2]{0:T(128)} %pad_add_fusion.me, f32[16,4,128]{2,1,0:T(4,128)} %copy-done.5, bf16[16,128,128]{2,1,0:T(8,128)(2,1)} %copy-done, bf16[16,128,128]{2,1,0:T(8,128)(2,1)} %copy-done.1), custom_call_target="tpu_custom_call" | custom-call | tf_op jit(solution)/shard_map/pallas_call | solution.py:34
  45.9 37.4 %all_to_all.40.got_ref = f32[24,8,128]{2,1,0:T(8,128)} all-to-all(f32[24,8,128]{2,1,0:T(8,128)} %get-tuple-element.16), channel_id=1, replica_groups=mesh['z_lo'=6,'x'=4,'col'=8,'z_hi'=2,'core'=2] {'z_lo','x'}, dimensions={0} | all-to-all | bytes 196608 | tf_op jit(solution)/shard_map/all_to_all | solution.py:29
  83.3 2.6 %shard_map.60 = f32[16,9,2,128]{3,2,1,0:T(2,128)} custom-call(s32[30]{0:T(128)} %pad_add_fusion.1.table, f32[24,8,128]{2,1,0:T(8,128)} %all_to_all.40.got_ref, bf16[16,128,128]{2,1,0:T(8,128)(2,1)} %copy-done, bf16[16,128,128]{2,1,0:T(8,128)(2,1)} %copy-done.1), custom_call_target="tpu_custom_call" | custom-call | tf_op jit(solution)/shard_map/pallas_call | solution.py:34
  85.8 1.9 collective-permute-start.2
  87.8 9.6 %all-to-all-start.2 = ((f32[16,9,2,128]{3,2,1,0:T(2,128)}), f32[16,9,2,128]{3,2,1,0:T(2,128)S(1)}, u32[]{:S(2)}, u32[]{:S(2)}) async-start(f32[16,9,2,128]{3,2,1,0:T(2,128)} %shard_map.60), calls=%async_computation.2 | async-start | bytes 294912 | tf_op jit(solution)/shard_map/all_to_all | solution.py:29
  97.4 0.7 pad_add_fusion.2.table
  98.1 14.8 %all-to-all-done.2.got_ref = f32[16,9,2,128]{3,2,1,0:T(2,128)S(1)} async-done(((f32[16,9,2,128]{3,2,1,0:T(2,128)}), f32[16,9,2,128]{3,2,1,0:T(2,128)S(1)}, u32[]{:S(2)}, u32[]{:S(2)}) %all-to-all-start.2) | async-done | bytes 147488 | tf_op jit(solution)/shard_map/all_to_all | solution.py:29
  112.9 0.6 copy-done.4
  113.5 2.9 %shard_map.61 = (f32[24,4,128]{2,1,0:T(4,128)}, f32[8,2,128]{2,1,0:T(2,128)}) custom-call(s32[60]{0:T(128)} %pad_add_fusion.2.table, s32[2]{0:T(128)} %pad_add_fusion.me, f32[8,4,128]{2,1,0:T(4,128)} %get-tuple-element.15.first_ref, f32[16,9,2,128]{3,2,1,0:T(2,128)} %copy-done.4, bf16[16,128,128]{2,1,0:T(8,128)(2,1)} %copy-done, ...), custom_call_target="tpu_custom_call" | custom-call | tf_op jit(solution)/shard_map/pallas_call | solution.py:34
  116.4 16.5 %all_to_all.41.got_ref = f32[24,4,128]{2,1,0:T(4,128)} all-to-all(f32[24,4,128]{2,1,0:T(4,128)} %get-tuple-element.19), channel_id=1, replica_groups=mesh['z_lo'=6,'x'=4,'col'=8,'z_hi'=2,'core'=2] {'z_lo','x'}, dimensions={0} | all-to-all | bytes 98304 | tf_op jit(solution)/shard_map/all_to_all | solution.py:29
  133.0 3.4 %shard_map.62 = f32[8,9,2,128]{3,2,1,0:T(2,128)} custom-call(s32[60]{0:T(128)} %pad_add_fusion.2.table, f32[24,4,128]{2,1,0:T(4,128)} %all_to_all.41.got_ref, bf16[16,128,128]{2,1,0:T(8,128)(2,1)} %copy-done, bf16[16,128,128]{2,1,0:T(8,128)(2,1)} %copy-done.1, bf16[16,128,128]{2,1,0:T(8,128)(2,1)} %copy-done.2, bf16[16,128,128]{2,1,0:T(8,128)(2,1)} %copy-done.3), custom_call_target="tpu_custom_call" | custom-call | tf_op jit(solution)/shard_map/pallas_call | solution.py:34
  136.3 12.4 %all_to_all.42.got_ref = f32[8,9,2,128]{3,2,1,0:T(2,128)} all-to-all(f32[8,9,2,128]{3,2,1,0:T(2,128)} %shard_map.62), channel_id=1, replica_groups=mesh['z_lo'=6,'x'=4,'col'=8,'z_hi'=2,'core'=2] {'col'}, dimensions={0} | all-to-all | bytes 147456 | tf_op jit(solution)/shard_map/all_to_all | solution.py:29
  148.8 2.9 %shard_map.63 = (f32[24,4,128]{2,1,0:T(4,128)}, f32[8,2,128]{2,1,0:T(2,128)}) custom-call(s32[60]{0:T(128)} %pad_add_fusion.2.table, s32[2]{0:T(128)} %pad_add_fusion.me, f32[8,4,128]{2,1,0:T(4,128)} %get-tuple-element.15.first_ref, f32[8,2,128]{2,1,0:T(2,128)} %get-tuple-element.18.last_ref, f32[8,9,2,128]{3,2,1,0:T(2,128)} %all_to_all.42.got_ref, ...), custom_call_target="tpu_custom_call" | custom-call | tf_op jit(solution)/shard_map/pallas_call | solution.py:34
  151.6 15.4 %all_to_all.43.got_ref = f32[24,4,128]{2,1,0:T(4,128)} all-to-all(f32[24,4,128]{2,1,0:T(4,128)} %get-tuple-element.21), channel_id=1, replica_groups=mesh['z_lo'=6,'x'=4,'col'=8,'z_hi'=2,'core'=2] {'z_lo','x'}, dimensions={0} | all-to-all | bytes 98304 | tf_op jit(solution)/shard_map/all_to_all | solution.py:29
  167.1 3.4 %shard_map.64 = (f32[8,3,2,128]{3,2,1,0:T(2,128)}, f32[2,128]{1,0:T(2,128)}) custom-call(s32[60]{0:T(128)} %pad_add_fusion.2.table, s32[2]{0:T(128)} %pad_add_fusion.me, f32[8,4,128]{2,1,0:T(4,128)} %get-tuple-element.15.first_ref, f32[8,2,128]{2,1,0:T(2,128)} %get-tuple-element.20.x_ref.x_all_ref, f32[24,4,128]{2,1,0:T(4,128)} %all_to_all.43.got_ref, ...), custom_call_target="tpu_custom_call" | custom-call | tf_op jit(solution)/shard_map/pallas_call | solution.py:34
  170.4 11.9 %all_to_all.44.got_ref = f32[8,3,2,128]{3,2,1,0:T(2,128)} all-to-all(f32[8,3,2,128]{3,2,1,0:T(2,128)} %get-tuple-element.23), channel_id=1, replica_groups=mesh['z_lo'=6,'x'=4,'col'=8,'z_hi'=2,'core'=2] {'col'}, dimensions={0} | all-to-all | bytes 49152 | tf_op jit(solution)/shard_map/all_to_all | solution.py:29
  182.3 1.4 shard_map.65
  183.7 15.4 %all_to_all.45.got_ref = f32[24,2,2,128]{3,2,1,0:T(2,128)} all-to-all(f32[24,2,2,128]{3,2,1,0:T(2,128)} %get-tuple-element.25), channel_id=1, replica_groups=mesh['z_lo'=6,'x'=4,'col'=8,'z_hi'=2,'core'=2] {'z_lo','x'}, dimensions={0} | all-to-all | bytes 98304 | tf_op jit(solution)/shard_map/all_to_all | solution.py:29
  199.1 1.5 shard_map.66
  200.6 0.7 copy-done.8
  201.3 0.6 slice_reduce_fusion
  (29 shorter events, 0.2 us)
Async XLA Ops:
  0.7 0.7 copy-start.7
  2.7 17.3 %copy-start.9 = (f32[128]{0:T(128)S(1)}, f32[128]{0:T(128)}, u32[]{:S(2)}) copy-start(f32[128]{0:T(128)} %param.5) | copy-start | bytes 1540
  2.8 40.2 %copy-start = (bf16[16,128,128]{2,1,0:T(8,128)(2,1)}, bf16[16,128,128]{2,1,0:T(8,128)(2,1)S(1)}, u32[]{:S(2)}) copy-start(bf16[16,128,128]{2,1,0:T(8,128)(2,1)S(1)} %pad_maximum_fusion.t0.refs_0_) | copy-start | bytes 1572868
  2.8 17.2 %copy-start.6 = (f32[2,128]{1,0:T(2,128)S(1)}, f32[2,128]{1,0:T(2,128)}, u32[]{:S(2)}) copy-start(f32[2,128]{1,0:T(2,128)} %param.4) | copy-start | bytes 3076
  2.8 25.8 %collective-permute-start = (bf16[16,128,128]{2,1,0:T(8,128)(2,1)S(1)}, bf16[16,128,128]{2,1,0:T(8,128)(2,1)S(1)}, u32[]{:S(2)}, u32[]{:S(2)}) collective-permute-start(bf16[16,128,128]{2,1,0:T(8,128)(2,1)S(1)} %pad_maximum_fusion.t0.refs_0_), channel_id=1, source_target_pairs={{0,1},{1,0},{2,3},{3,2},{4,5},{5,4},{6,7},{7,6},{8,9},{9,8},{10,11... | collective-permute-start | bytes 1572872 | tf_op jit(solution)/shard_map/ppermute | solution.py:218
  4.8 81.0 %collective-permute-start.1 = (bf16[16,128,128]{2,1,0:T(8,128)(2,1)S(1)}, bf16[16,128,128]{2,1,0:T(8,128)(2,1)S(1)}, u32[]{:S(2)}, u32[]{:S(2)}) collective-permute-start(bf16[16,128,128]{2,1,0:T(8,128)(2,1)S(1)} %pad_maximum_fusion.t0.refs_0_), channel_id=1, source_target_pairs={{0,2},{2,0},{1,3},{3,1},{4,6},{6,4},{5,7},{7,5},{8,10},{10,8},{9,1... | collective-permute-start | bytes 1572872 | tf_op jit(solution)/shard_map/ppermute | solution.py:217
  20.6 22.3 %all-to-all-start = ((f32[16,4,128]{2,1,0:T(4,128)}), f32[16,4,128]{2,1,0:T(4,128)S(1)}, u32[]{:S(2)}, u32[]{:S(2)}) async-start(f32[16,4,128]{2,1,0:T(4,128)} %broadcast_in_dim.15), calls=%async_computation | async-start | bytes 65536 | tf_op jit(solution)/shard_map/all_to_all | solution.py:29
  28.5 14.5 %copy-start.1 = (bf16[16,128,128]{2,1,0:T(8,128)(2,1)}, bf16[16,128,128]{2,1,0:T(8,128)(2,1)S(1)}, u32[]{:S(2)}) copy-start(bf16[16,128,128]{2,1,0:T(8,128)(2,1)S(1)} %collective-permute-done.t1.refs_1_) | copy-start | bytes 1572868
  43.0 0.6 copy-start.5
  85.8 27.0 %copy-start.2 = (bf16[16,128,128]{2,1,0:T(8,128)(2,1)}, bf16[16,128,128]{2,1,0:T(8,128)(2,1)S(1)}, u32[]{:S(2)}) copy-start(bf16[16,128,128]{2,1,0:T(8,128)(2,1)S(1)} %collective-permute-done.1.t2.refs_2_) | copy-start | bytes 1572868
  85.8 11.5 %collective-permute-start.2 = (bf16[16,128,128]{2,1,0:T(8,128)(2,1)S(1)}, bf16[16,128,128]{2,1,0:T(8,128)(2,1)S(1)}, u32[]{:S(2)}, u32[]{:S(2)}) collective-permute-start(bf16[16,128,128]{2,1,0:T(8,128)(2,1)S(1)} %collective-permute-done.1.t2.refs_2_), channel_id=1, source_target_pairs={{0,1},{1,0},{2,3},{3,2},{4,5},{5,4},{6,7},{7,6},{8,9},{9,8},{10,11... | collective-permute-start | bytes 1572872 | tf_op jit(solution)/shard_map/ppermute | solution.py:247
  87.8 25.1 %all-to-all-start.2 = ((f32[16,9,2,128]{3,2,1,0:T(2,128)}), f32[16,9,2,128]{3,2,1,0:T(2,128)S(1)}, u32[]{:S(2)}, u32[]{:S(2)}) async-start(f32[16,9,2,128]{3,2,1,0:T(2,128)} %shard_map.60), calls=%async_computation.2 | async-start | bytes 294912 | tf_op jit(solution)/shard_map/all_to_all | solution.py:29
  97.4 15.5 %copy-start.3 = (bf16[16,128,128]{2,1,0:T(8,128)(2,1)}, bf16[16,128,128]{2,1,0:T(8,128)(2,1)S(1)}, u32[]{:S(2)}) copy-start(bf16[16,128,128]{2,1,0:T(8,128)(2,1)S(1)} %collective-permute-done.2.t3.refs_3_) | copy-start | bytes 1572868
  112.9 0.7 copy-start.4
  200.6 0.7 copy-start.8

commit v3 on v2

v3 whole, which is shorter than its diff:
```python
import jax
import jax.numpy as jnp
from jax import lax
from jax.experimental import pallas as pl
from jax.experimental.pallas import tpu as pltpu
from jax.sharding import Mesh
from jax.sharding import PartitionSpec as P

ROW = ("z_lo", "x")
COL = ("col", "z_hi")
REP = ("z_hi", "core")
ROW_COL = ("z_lo", "x", "col")
ROW_COL_REP = ("z_lo", "x", "col", "z_hi", "core")

filter_low = 5.0
filter_top = 20.0
spectrum_low = -3.0

half = (filter_top - filter_low) / 2.0
centre = (filter_top + filter_low) / 2.0
sigma_first = half / (spectrum_low - centre)
tau_value = 2.0 / sigma_first
sigma_next = 1.0 / (tau_value - sigma_first)

VMEM = pl.BlockSpec(memory_space=pltpu.VMEM)
SMEM = pl.BlockSpec(memory_space=pltpu.SMEM)


def exchange(blocks, axis):
    return lax.all_to_all(blocks, axis, 0, 0, tiled=True)


def call(body, out_shapes, scalars, arrays, scratch=()):
    arrays = [pltpu.with_memory_space_constraint(a, pltpu.VMEM) for a in arrays]
    return pl.pallas_call(
        body,
        out_shape=[pltpu.VMEM(shape, jnp.float32) for shape in out_shapes],
        in_specs=[SMEM] * len(scalars) + [VMEM] * len(arrays),
        out_specs=[VMEM] * len(out_shapes),
        scratch_shapes=[pltpu.VMEM(shape, jnp.float32) for shape in scratch],
    )(*scalars, *arrays)


def place(code, rows):
    shift = 16
    a = (code * (-(-(1 << shift) // rows))) >> shift
    return a, code - a * rows


def mirror_products(codes, me, x_ref, tile_refs, send_ref):
    rows, vecs = send_ref.shape[0], x_ref.shape[1]
    slots = tile_refs[0].shape[0]
    own = x_ref[me]
    for k in range(rows):
        send_ref[k, :vecs, :] = jnp.zeros_like(own)
        send_ref[k, vecs:, :] = own
    for group, tiles in enumerate(tile_refs):
        for slot in range(slots):
            a, k = place(codes[group * slots + slot], rows)
            part = lax.dot_general(
                x_ref[a].astype(jnp.bfloat16),
                tiles[slot],
                (((1,), (0,)), ((), ())),
                preferred_element_type=jnp.float32,
            )
            send_ref[k, :vecs, :] += part


def direct_products(codes, me, got_ref, tile_refs, sums_ref):
    vecs = sums_ref.shape[1]
    rows = got_ref.shape[0]
    slots = tile_refs[0].shape[0]
    mirror = got_ref[0, :vecs, :]
    for k in range(1, rows):
        mirror = mirror + got_ref[k, :vecs, :]
    sums_ref[...] = jnp.zeros_like(sums_ref)
    sums_ref[me] = mirror
    for group, tiles in enumerate(tile_refs):
        for slot in range(slots):
            a, k = place(codes[group * slots + slot], rows)
            part = lax.dot_general(
                got_ref[k, vecs:, :].astype(jnp.bfloat16),
                tiles[slot],
                (((1,), (1,)), ((), ())),
                preferred_element_type=jnp.float32,
            )
            sums_ref[a] += part


def summed(got_ref, a):
    total = got_ref[0, a]
    for peer in range(1, got_ref.shape[0]):
        total = total + got_ref[peer, a]
    return total


def start_kernel(codes, me, first_ref, t0, t1, send_ref, base_ref):
    cols = base_ref.shape[1]
    halves = first_ref.shape[0] // cols
    vecs = first_ref.shape[1] // 2
    for a in range(cols):
        for z in range(halves):
            part = slice(z * vecs, (z + 1) * vecs)
            base_ref[0, a, part, :] = first_ref[a * halves + z, :vecs, :]
            base_ref[1, a, part, :] = first_ref[a * halves + z, vecs:, :]
    mirror_products(codes, me[0], base_ref.at[0], (t0, t1), send_ref)


def second_kernel(codes, me, base_ref, got_ref, t0, t1, send_ref, x_ref):
    for a in range(x_ref.shape[0]):
        x = base_ref[0, a]
        image = base_ref[1, a] * x + summed(got_ref, a)
        x_ref[a] = (image - centre * x) * (sigma_first / half)
    mirror_products(codes, me[0], x_ref, (t0, t1), send_ref)


def third_kernel(codes, me, base_ref, last_ref, got_ref, t0, t1, send_ref, x_ref):
    for a in range(x_ref.shape[0]):
        x = last_ref[a]
        image = base_ref[1, a] * x + summed(got_ref, a)
        x_ref[a] = (image - centre * x) * (2.0 * sigma_next / half) - (
            sigma_first * sigma_next
        ) * base_ref[0, a]
    mirror_products(codes, me[0], x_ref, (t0, t1), send_ref)


def direct_kernel(codes, me, got_ref, t0, t1, send_ref, sums_ref):
    direct_products(codes, me[0], got_ref, (t0, t1), sums_ref)
    for peer in range(send_ref.shape[0]):
        send_ref[peer] = sums_ref[...]


def last_direct_kernel(codes, me, base_ref, x_ref, got_ref, t0, t1, send_ref, sums_ref):
    direct_products(codes, me[0], got_ref, (t0, t1), sums_ref)
    cols, vecs = sums_ref.shape[0], send_ref.shape[1] // 3
    halves = send_ref.shape[0] // cols
    x = x_ref[me[0]]
    energy = base_ref[1, me[0]]
    crossed = x_ref[0] * sums_ref[0]
    for a in range(1, cols):
        crossed = crossed + x_ref[a] * sums_ref[a]
    for z in range(halves):
        part = slice(z * vecs, (z + 1) * vecs)
        once = jnp.where(me[1] == z, 1.0, 0.0)
        square = x[part] * x[part] * once
        local = crossed[part] + energy[part] * square
        for c in range(cols):
            send_ref[c * halves + z, :vecs, :] = sums_ref[c, part, :]
            send_ref[c * halves + z, vecs : 2 * vecs, :] = local
            send_ref[c * halves + z, 2 * vecs :, :] = square


def own_part(ref, index, half_index, vecs):
    block = ref[index]
    part = block[:vecs]
    for z in range(1, block.shape[0] // vecs):
        part = jnp.where(half_index == z, block[z * vecs : (z + 1) * vecs], part)
    return part


def image_kernel(got_ref, image_ref, send_ref):
    vecs = image_ref.shape[0]
    total = got_ref[0]
    for peer in range(1, got_ref.shape[0]):
        total = total + got_ref[peer]
    image_ref[...] = total[:vecs]
    for k in range(send_ref.shape[0]):
        send_ref[k] = total[vecs:]


def correct_kernel(me, base_ref, x_ref, image_ref, got_ref, out_ref, ritz_ref):
    vecs = out_ref.shape[0]
    total = got_ref[0]
    for k in range(1, got_ref.shape[0]):
        total = total + got_ref[k]
    total = jnp.sum(total, axis=1, keepdims=True)
    ritz = total[:vecs] / (total[vecs:] + 1e-06)
    x = own_part(x_ref, me[0], me[1], vecs)
    energy = base_ref[1, me[0]][:vecs]
    resid = energy * x + image_ref[...] - ritz * x
    spacing = energy - ritz
    out_ref[...] = x - spacing / jnp.maximum(spacing * spacing, 1.0) * resid
    ritz_ref[...] = jnp.broadcast_to(ritz, ritz_ref.shape)


def on_device(vectors, energies, tiles, tile_codes):
    rows = lax.axis_size(ROW)
    cols = lax.axis_size("col")
    halves = lax.axis_size("z_hi")
    row_index = lax.axis_index(ROW)
    col_index = lax.axis_index("col")
    half_index = lax.axis_index("z_hi")
    slots, side = tiles.shape[0], tiles.shape[1]
    vecs = vectors.shape[0]
    wide = vecs * halves
    present = tile_codes >= 0
    safe_code = jnp.where(present, tile_codes, 0)
    on_diagonal = present & (safe_code == col_index * rows + row_index)
    upper_mask = lax.broadcasted_iota(jnp.int32, (side, side), 1) > lax.broadcasted_iota(
        jnp.int32, (side, side), 0
    )
    keep_mask = present[:, None, None] & (
        upper_mask[None] | jnp.logical_not(on_diagonal)[:, None, None]
    )
    stored = jnp.where(keep_mask, tiles, jnp.zeros((), tiles.dtype))
    swap = [(0, 1), (1, 0)]
    near = lax.ppermute(stored, "core", swap)
    near_code = lax.ppermute(safe_code, "core", swap)
    codes = jnp.concatenate([safe_code, near_code])
    pair = (stored, near)

    first = jnp.concatenate([vectors, jnp.broadcast_to(energies[None], (vecs, side))], axis=0)
    first = exchange(jnp.broadcast_to(first[None], (cols * halves, *first.shape)), COL)
    me = jnp.stack([col_index, half_index]).astype(jnp.int32)

    row_shape = (rows, 2 * wide, side)
    state_shape = (cols, wide, side)
    col_shape = (cols * halves, cols, wide, side)
    scalars = (codes, me)

    def col_step(got):
        (send,) = call(direct_kernel, [col_shape], scalars, (got, *pair), [state_shape])
        return exchange(send, COL)

    send, base = call(start_kernel, [row_shape, (2, *state_shape)], scalars, (first, *pair))
    got = col_step(exchange(send, ROW))
    send, x1 = call(second_kernel, [row_shape, state_shape], scalars, (base, got, *pair))
    got = col_step(exchange(send, ROW))
    send, x2 = call(third_kernel, [row_shape, state_shape], scalars, (base, x1, got, *pair))
    got = exchange(send, ROW)
    (send,) = call(
        last_direct_kernel,
        [(cols * halves, 3 * vecs, side)],
        scalars,
        (base, x2, got, *pair),
        [state_shape],
    )
    got = exchange(send, COL)
    image, send = call(image_kernel, [(vecs, side), (rows, 2 * vecs, side)], (), (got,))
    got = exchange(send, ROW)
    out, ritz = call(
        correct_kernel, [(vecs, side), (vecs, side)], (me,), (base, x2, image, got)
    )
    return out, ritz[:, 0]


def solution(mesh):
    split = Mesh(
        mesh.devices.reshape(6, 4, mesh.shape["col"], 2, 2),
        ("z_lo", "x", "col", "z_hi", "core"),
    )
    return jax.shard_map(
        on_device,
        mesh=split,
        in_specs=(P(REP, ROW_COL), P(ROW_COL), P(ROW_COL_REP, None, None), P(ROW_COL_REP)),
        out_specs=(P(REP, ROW_COL), P(REP)),
        check_vma=False,
    )
```

time: 203 us -> 176 us (0.87)
  waiting for transfers between devices: 28.6 us -> 13.7 us
  blocking collectives: 109 us -> 123 us
  Pallas kernels: 20.3 us -> 8.07 us
  starting transfers between devices: 35.9 us -> 24.2 us
    all_to_all x2 -> x1, waiting for transfers between devices: 28.6 us -> 13.7 us  [exchange(): return lax.all_to_all(blocks, axis, 0, 0, tiled=True)]
    ppermute x2 -> x1, starting transfers between devices: 17 us -> 2.41 us  [on_device(): near_code = lax.ppermute(safe_code, 'core', swap)]
    all_to_all x6 -> x7, blocking collectives: 109 us -> 123 us  [exchange(): return lax.all_to_all(blocks, axis, 0, 0, tiled=True)]
    pallas_call x8, Pallas kernels: 20.3 us -> 8.07 us  [call(): pl.pallas_call(body, out_shape=[pltpu.VMEM(shape, jnp.float32) for shape...]
    all_to_all x2 -> x1, starting transfers between devices: 16.8 us -> 19.9 us  [exchange(): return lax.all_to_all(blocks, axis, 0, 0, tiled=True)]
  transfers between devices with their start and end apart: 5 -> 3, of which waited for: 2 -> 1; matrix products, arithmetic and copies ran while one was open for 1% -> 1% of each run, Pallas kernels for 2% -> 0%
where the time goes in v3:
time: 176 us; the launch traced here: 175 us
  blocking collectives  123 us (70%)
  starting transfers between devices  24.2 us (14%)
  waiting for transfers between devices  13.7 us (8%)
  Pallas kernels  8.07 us (5%)
  other arithmetic  2.54 us (1%)
  local copies, waits for them, and re-layouts  2.48 us (1%)
    all_to_all x7, blocking collectives, exchange(): return lax.all_to_all(blocks, axis, 0, 0, tiled=True)  123 us
    all_to_all x1, starting transfers between devices, exchange(): return lax.all_to_all(blocks, axis, 0, 0, tiled=True)  19.9 us
    all_to_all x1, waiting for transfers between devices, exchange(): return lax.all_to_all(blocks, axis, 0, 0, tiled=True)  13.7 us
    pallas_call x8, Pallas kernels, call(): pl.pallas_call(body, out_shape=[pltpu.VMEM(shape, jnp.float32) for shape...  8.07 us
  transfers between devices with their start and end apart: 3, of which 1 were waited for; matrix products, arithmetic and copies ran while one was open for 1% of the time, Pallas kernels for 0%

profile of v3, /device:TPU:2, one launch (start us, length us, event | category | flops | bytes accessed | tf_op | source)
XLA Modules:
  0.0 174.9 jit_solution(15243292809814551456)
XLA Ops:
  0.7 0.0 copy-start.1
  0.7 0.6 copy-done.1
  1.3 1.3 and_select_fusion.t0
  2.7 0.0 copy-start.2
  2.7 1.9 %collective-permute-start.1 = (bf16[15,128,128]{2,1,0:T(8,128)(2,1)S(1)}, bf16[15,128,128]{2,1,0:T(8,128)(2,1)S(1)}, u32[]{:S(2)}, u32[]{:S(2)}) collective-permute-start(bf16[15,128,128]{2,1,0:T(8,128)(2,1)S(1)} %and_select_fusion.t0), channel_id=1, source_target_pairs={{0,1},{1,0},{2,3},{3,2},{4,5},{5,4},{6,7},{7,6},{8,9},{9,8},{10,11... | collective-permute-start | bytes 1474568 | tf_op jit(solution)/shard_map/ppermute | solution.py:207
  4.6 0.0 copy-start
  4.6 2.4 %collective-permute-start = (s32[15]{0:T(128)S(1)}, s32[15]{0:T(128)S(1)}, u32[]{:S(2)}, u32[]{:S(2)}) collective-permute-start(s32[15]{0:T(128)S(1)} %broadcast_select_fusion), channel_id=1, source_target_pairs={{0,1},{1,0},{2,3},{3,2},{4,5},{5,4},{6,7},{7,6},{8,9},{9,8},{10,11... | collective-permute-start | bytes 188 | tf_op jit(solution)/shard_map/ppermute | solution.py:208
  7.0 0.0 copy-done.2
  7.1 0.0 copy-done
  7.1 0.6 broadcast_in_dim.11
  7.7 19.9 %all-to-all-start = ((f32[16,4,128]{2,1,0:T(4,128)}), f32[16,4,128]{2,1,0:T(4,128)S(1)}, u32[]{:S(2)}, u32[]{:S(2)}) async-start(f32[16,4,128]{2,1,0:T(4,128)} %broadcast_in_dim.11), calls=%async_computation | async-start | bytes 65536 | tf_op jit(solution)/shard_map/all_to_all | solution.py:30
  27.6 0.6 pad_add_fusion.me
  28.2 0.0 collective-permute-done
  28.2 0.6 pad_add_fusion.1.codes
  28.8 13.7 %all-to-all-done.first_ref = f32[16,4,128]{2,1,0:T(4,128)S(1)} async-done(((f32[16,4,128]{2,1,0:T(4,128)}), f32[16,4,128]{2,1,0:T(4,128)S(1)}, u32[]{:S(2)}, u32[]{:S(2)}) %all-to-all-start) | async-done | bytes 32800 | tf_op jit(solution)/shard_map/all_to_all | solution.py:30
  42.5 0.0 collective-permute-done.1.t1
  42.5 1.1 shard_map.59
  43.6 18.9 %all_to_all.40.got_ref = f32[24,8,128]{2,1,0:T(8,128)S(1)} all-to-all(f32[24,8,128]{2,1,0:T(8,128)S(1)} %get-tuple-element.13), channel_id=1, replica_groups=mesh['z_lo'=6,'x'=4,'col'=8,'z_hi'=2,'core'=2] {'z_lo','x'}, dimensions={0} | all-to-all | bytes 196608 | tf_op jit(solution)/shard_map/all_to_all | solution.py:30
  62.5 1.3 shard_map.60
  63.9 18.6 %all_to_all.41.got_ref = f32[16,8,4,128]{3,2,1,0:T(4,128)S(1)} all-to-all(f32[16,8,4,128]{3,2,1,0:T(4,128)S(1)} %shard_map.60), channel_id=1, replica_groups=mesh['z_lo'=6,'x'=4,'col'=8,'z_hi'=2,'core'=2] {'col','z_hi'}, dimensions={0} | all-to-all | bytes 524288 | tf_op jit(solution)/shard_map/all_to_all | solution.py:30
  82.4 1.1 shard_map.61
  83.5 17.0 %all_to_all.42.got_ref = f32[24,8,128]{2,1,0:T(8,128)S(1)} all-to-all(f32[24,8,128]{2,1,0:T(8,128)S(1)} %get-tuple-element.15), channel_id=1, replica_groups=mesh['z_lo'=6,'x'=4,'col'=8,'z_hi'=2,'core'=2] {'z_lo','x'}, dimensions={0} | all-to-all | bytes 196608 | tf_op jit(solution)/shard_map/all_to_all | solution.py:30
  100.5 1.3 shard_map.62
  101.9 19.6 %all_to_all.43.got_ref = f32[16,8,4,128]{3,2,1,0:T(4,128)S(1)} all-to-all(f32[16,8,4,128]{3,2,1,0:T(4,128)S(1)} %shard_map.62), channel_id=1, replica_groups=mesh['z_lo'=6,'x'=4,'col'=8,'z_hi'=2,'core'=2] {'col','z_hi'}, dimensions={0} | all-to-all | bytes 524288 | tf_op jit(solution)/shard_map/all_to_all | solution.py:30
  121.5 1.1 shard_map.63
  122.6 16.6 %all_to_all.44.got_ref = f32[24,8,128]{2,1,0:T(8,128)S(1)} all-to-all(f32[24,8,128]{2,1,0:T(8,128)S(1)} %get-tuple-element.17), channel_id=1, replica_groups=mesh['z_lo'=6,'x'=4,'col'=8,'z_hi'=2,'core'=2] {'z_lo','x'}, dimensions={0} | all-to-all | bytes 196608 | tf_op jit(solution)/shard_map/all_to_all | solution.py:30
  139.2 1.3 shard_map.64
  140.5 17.8 %all_to_all.45.got_ref = f32[16,6,128]{2,1,0:T(8,128)S(1)} all-to-all(f32[16,6,128]{2,1,0:T(8,128)S(1)} %shard_map.64), channel_id=1, replica_groups=mesh['z_lo'=6,'x'=4,'col'=8,'z_hi'=2,'core'=2] {'col','z_hi'}, dimensions={0} | all-to-all | bytes 98304 | tf_op jit(solution)/shard_map/all_to_all | solution.py:30
  158.4 14.5 %all_to_all.46.got_ref = f32[24,4,128]{2,1,0:T(4,128)S(1)} all-to-all(f32[24,4,128]{2,1,0:T(4,128)S(1)} %get-tuple-element.19), channel_id=1, replica_groups=mesh['z_lo'=6,'x'=4,'col'=8,'z_hi'=2,'core'=2] {'z_lo','x'}, dimensions={0} | all-to-all | bytes 98304 | tf_op jit(solution)/shard_map/all_to_all | solution.py:30
  172.9 0.8 shard_map.66
  173.7 0.6 copy.6
  174.3 0.6 slice_reduce_fusion
  (6 shorter events, 0.1 us)
Async XLA Ops:
  0.7 0.7 copy-start.1
  2.7 4.4 %copy-start.2 = (f32[128]{0:T(128)S(1)}, f32[128]{0:T(128)}, u32[]{:S(2)}) copy-start(f32[128]{0:T(128)} %param.5) | copy-start | bytes 1540
  2.7 39.9 %collective-permute-start.1 = (bf16[15,128,128]{2,1,0:T(8,128)(2,1)S(1)}, bf16[15,128,128]{2,1,0:T(8,128)(2,1)S(1)}, u32[]{:S(2)}, u32[]{:S(2)}) collective-permute-start(bf16[15,128,128]{2,1,0:T(8,128)(2,1)S(1)} %and_select_fusion.t0), channel_id=1, source_target_pairs={{0,1},{1,0},{2,3},{3,2},{4,5},{5,4},{6,7},{7,6},{8,9},{9,8},{10,11... | collective-permute-start | bytes 1474568 | tf_op jit(solution)/shard_map/ppermute | solution.py:207
  4.6 2.4 %copy-start = (f32[2,128]{1,0:T(2,128)S(1)}, f32[2,128]{1,0:T(2,128)}, u32[]{:S(2)}) copy-start(f32[2,128]{1,0:T(2,128)} %param.4) | copy-start | bytes 3076
  4.6 23.6 %collective-permute-start = (s32[15]{0:T(128)S(1)}, s32[15]{0:T(128)S(1)}, u32[]{:S(2)}, u32[]{:S(2)}) collective-permute-start(s32[15]{0:T(128)S(1)} %broadcast_select_fusion), channel_id=1, source_target_pairs={{0,1},{1,0},{2,3},{3,2},{4,5},{5,4},{6,7},{7,6},{8,9},{9,8},{10,11... | collective-permute-start | bytes 188 | tf_op jit(solution)/shard_map/ppermute | solution.py:208
  7.7 34.8 %all-to-all-start = ((f32[16,4,128]{2,1,0:T(4,128)}), f32[16,4,128]{2,1,0:T(4,128)S(1)}, u32[]{:S(2)}, u32[]{:S(2)}) async-start(f32[16,4,128]{2,1,0:T(4,128)} %broadcast_in_dim.11), calls=%async_computation | async-start | bytes 65536 | tf_op jit(solution)/shard_map/all_to_all | solution.py:30

commit v4 on v3

--- a/solution.py
+++ b/solution.py
@@ -30,11 +30,12 @@
     return lax.all_to_all(blocks, axis, 0, 0, tiled=True)
 
 
-def call(body, out_shapes, scalars, arrays, scratch=()):
-    arrays = [pltpu.with_memory_space_constraint(a, pltpu.VMEM) for a in arrays]
+def call(body, out_shapes, scalars, arrays, scratch=(), space=pltpu.VMEM, hold=True):
+    if hold:
+        arrays = [pltpu.with_memory_space_constraint(a, pltpu.VMEM) for a in arrays]
     return pl.pallas_call(
         body,
-        out_shape=[pltpu.VMEM(shape, jnp.float32) for shape in out_shapes],
+        out_shape=[space(shape, jnp.float32) for shape in out_shapes],
         in_specs=[SMEM] * len(scalars) + [VMEM] * len(arrays),
         out_specs=[VMEM] * len(out_shapes),
         scratch_shapes=[pltpu.VMEM(shape, jnp.float32) for shape in scratch],
@@ -94,6 +95,14 @@
     return total
 
 
+def spread_kernel(vectors_ref, energies_ref, send_ref):
+    vecs = vectors_ref.shape[0]
+    energy = jnp.broadcast_to(energies_ref[...], vectors_ref.shape)
+    for peer in range(send_ref.shape[0]):
+        send_ref[peer, :vecs, :] = vectors_ref[...]
+        send_ref[peer, vecs:, :] = energy
+
+
 def start_kernel(codes, me, first_ref, t0, t1, send_ref, base_ref):
     cols = base_ref.shape[1]
     halves = first_ref.shape[0] // cols
@@ -180,7 +189,11 @@
     resid = energy * x + image_ref[...] - ritz * x
     spacing = energy - ritz
     out_ref[...] = x - spacing / jnp.maximum(spacing * spacing, 1.0) * resid
-    ritz_ref[...] = jnp.broadcast_to(ritz, ritz_ref.shape)
+    row = jnp.broadcast_to(ritz[:1], (1, x.shape[1]))
+    lane = lax.broadcasted_iota(jnp.int32, row.shape, 1)
+    for v in range(1, vecs):
+        row = jnp.where(lane == v, ritz[v : v + 1], row)
+    ritz_ref[...] = row[:, :vecs]
 
 
 def on_device(vectors, energies, tiles, tile_codes):
@@ -190,7 +203,7 @@
     row_index = lax.axis_index(ROW)
     col_index = lax.axis_index("col")
     half_index = lax.axis_index("z_hi")
-    slots, side = tiles.shape[0], tiles.shape[1]
+    side = tiles.shape[1]
     vecs = vectors.shape[0]
     wide = vecs * halves
     present = tile_codes >= 0
@@ -209,8 +222,14 @@
     codes = jnp.concatenate([safe_code, near_code])
     pair = (stored, near)
 
-    first = jnp.concatenate([vectors, jnp.broadcast_to(energies[None], (vecs, side))], axis=0)
-    first = exchange(jnp.broadcast_to(first[None], (cols * halves, *first.shape)), COL)
+    (first,) = call(
+        spread_kernel,
+        [(cols * halves, 2 * vecs, side)],
+        (),
+        (vectors, energies[None]),
+        hold=False,
+    )
+    first = exchange(first, COL)
     me = jnp.stack([col_index, half_index]).astype(jnp.int32)
 
     row_shape = (rows, 2 * wide, side)
@@ -239,9 +258,13 @@
     image, send = call(image_kernel, [(vecs, side), (rows, 2 * vecs, side)], (), (got,))
     got = exchange(send, ROW)
     out, ritz = call(
-        correct_kernel, [(vecs, side), (vecs, side)], (me,), (base, x2, image, got)
-    )
-    return out, ritz[:, 0]
+        correct_kernel,
+        [(vecs, side), (1, vecs)],
+        (me,),
+        (base, x2, image, got),
+        space=jax.ShapeDtypeStruct,
+    )
+    return out, ritz[0]
 
 
 def solution(mesh):

time: 176 us -> 176 us (level)
  Pallas kernels: 8.07 us -> 9.98 us
  local copies, waits for them, and re-layouts: 2.48 us -> 0.65 us
    pallas_call x8 -> x9, Pallas kernels: 8.07 us -> 9.98 us  [call(): pl.pallas_call(body, out_shape=[space(shape, jnp.float32) for shape in ou...]
  transfers between devices with their start and end apart: 3 -> 3, of which waited for: 1 -> 1; matrix products, arithmetic and copies ran while one was open for 1% -> 1% of each run, Pallas kernels for 0% -> 1%
where the time goes in v4:
time: 176 us; the launch traced here: 175 us
  blocking collectives  123 us (70%)
  starting transfers between devices  24.2 us (14%)
  waiting for transfers between devices  13.7 us (8%)
  Pallas kernels  9.98 us (6%)
  other arithmetic  2.53 us (1%)
    all_to_all x7, blocking collectives, exchange(): return lax.all_to_all(blocks, axis, 0, 0, tiled=True)  123 us
    all_to_all x1, starting transfers between devices, exchange(): return lax.all_to_all(blocks, axis, 0, 0, tiled=True)  19.9 us
    all_to_all x1, waiting for transfers between devices, exchange(): return lax.all_to_all(blocks, axis, 0, 0, tiled=True)  13.7 us
    pallas_call x9, Pallas kernels, call(): pl.pallas_call(body, out_shape=[space(shape, jnp.float32) for shape in ou...  9.98 us
  transfers between devices with their start and end apart: 3, of which 1 were waited for; matrix products, arithmetic and copies ran while one was open for 1% of the time, Pallas kernels for 1%

profile of v4, /device:TPU:2, one launch (start us, length us, event | category | flops | bytes accessed | tf_op | source)
XLA Modules:
  0.0 174.9 jit_solution(2242522893341405477)
XLA Ops:
  0.7 0.0 copy-start
  0.7 0.6 copy-done
  1.3 1.3 and_select_fusion.t0
  2.7 1.9 %collective-permute-start.1 = (bf16[15,128,128]{2,1,0:T(8,128)(2,1)S(1)}, bf16[15,128,128]{2,1,0:T(8,128)(2,1)S(1)}, u32[]{:S(2)}, u32[]{:S(2)}) collective-permute-start(bf16[15,128,128]{2,1,0:T(8,128)(2,1)S(1)} %and_select_fusion.t0), channel_id=1, source_target_pairs={{0,1},{1,0},{2,3},{3,2},{4,5},{5,4},{6,7},{7,6},{8,9},{9,8},{10,11... | collective-permute-start | bytes 1474568 | tf_op jit(solution)/shard_map/ppermute | solution.py:220
  4.6 2.4 %collective-permute-start = (s32[15]{0:T(128)S(1)}, s32[15]{0:T(128)S(1)}, u32[]{:S(2)}, u32[]{:S(2)}) collective-permute-start(s32[15]{0:T(128)S(1)} %broadcast_select_fusion), channel_id=1, source_target_pairs={{0,1},{1,0},{2,3},{3,2},{4,5},{5,4},{6,7},{7,6},{8,9},{9,8},{10,11... | collective-permute-start | bytes 188 | tf_op jit(solution)/shard_map/ppermute | solution.py:221
  7.0 1.3 shard_map.59
  8.3 19.9 %all-to-all-start = ((f32[16,4,128]{2,1,0:T(4,128)}), f32[16,4,128]{2,1,0:T(4,128)S(1)}, u32[]{:S(2)}, u32[]{:S(2)}) async-start(f32[16,4,128]{2,1,0:T(4,128)} %shard_map.59), calls=%async_computation | async-start | bytes 65536 | tf_op jit(solution)/shard_map/all_to_all | solution.py:30
  28.2 0.6 pad_add_fusion.me
  28.8 0.0 collective-permute-done
  28.8 0.6 pad_add_fusion.1.codes
  29.4 13.7 %all-to-all-done.first_ref = f32[16,4,128]{2,1,0:T(4,128)S(1)} async-done(((f32[16,4,128]{2,1,0:T(4,128)}), f32[16,4,128]{2,1,0:T(4,128)S(1)}, u32[]{:S(2)}, u32[]{:S(2)}) %all-to-all-start) | async-done | bytes 32800 | tf_op jit(solution)/shard_map/all_to_all | solution.py:30
  43.1 0.0 collective-permute-done.1.t1
  43.1 1.1 shard_map.60
  44.2 18.9 %all_to_all.40.got_ref = f32[24,8,128]{2,1,0:T(8,128)S(1)} all-to-all(f32[24,8,128]{2,1,0:T(8,128)S(1)} %get-tuple-element.13), channel_id=1, replica_groups=mesh['z_lo'=6,'x'=4,'col'=8,'z_hi'=2,'core'=2] {'z_lo','x'}, dimensions={0} | all-to-all | bytes 196608 | tf_op jit(solution)/shard_map/all_to_all | solution.py:30
  63.1 1.3 shard_map.61
  64.5 18.6 %all_to_all.41.got_ref = f32[16,8,4,128]{3,2,1,0:T(4,128)S(1)} all-to-all(f32[16,8,4,128]{3,2,1,0:T(4,128)S(1)} %shard_map.61), channel_id=1, replica_groups=mesh['z_lo'=6,'x'=4,'col'=8,'z_hi'=2,'core'=2] {'col','z_hi'}, dimensions={0} | all-to-all | bytes 524288 | tf_op jit(solution)/shard_map/all_to_all | solution.py:30
  83.1 1.1 shard_map.62
  84.1 17.0 %all_to_all.42.got_ref = f32[24,8,128]{2,1,0:T(8,128)S(1)} all-to-all(f32[24,8,128]{2,1,0:T(8,128)S(1)} %get-tuple-element.15), channel_id=1, replica_groups=mesh['z_lo'=6,'x'=4,'col'=8,'z_hi'=2,'core'=2] {'z_lo','x'}, dimensions={0} | all-to-all | bytes 196608 | tf_op jit(solution)/shard_map/all_to_all | solution.py:30
  101.1 1.3 shard_map.63
  102.5 19.6 %all_to_all.43.got_ref = f32[16,8,4,128]{3,2,1,0:T(4,128)S(1)} all-to-all(f32[16,8,4,128]{3,2,1,0:T(4,128)S(1)} %shard_map.63), channel_id=1, replica_groups=mesh['z_lo'=6,'x'=4,'col'=8,'z_hi'=2,'core'=2] {'col','z_hi'}, dimensions={0} | all-to-all | bytes 524288 | tf_op jit(solution)/shard_map/all_to_all | solution.py:30
  122.1 1.1 shard_map.64
  123.2 16.6 %all_to_all.44.got_ref = f32[24,8,128]{2,1,0:T(8,128)S(1)} all-to-all(f32[24,8,128]{2,1,0:T(8,128)S(1)} %get-tuple-element.17), channel_id=1, replica_groups=mesh['z_lo'=6,'x'=4,'col'=8,'z_hi'=2,'core'=2] {'z_lo','x'}, dimensions={0} | all-to-all | bytes 196608 | tf_op jit(solution)/shard_map/all_to_all | solution.py:30
  139.8 1.3 shard_map.65
  141.1 17.8 %all_to_all.45.got_ref = f32[16,6,128]{2,1,0:T(8,128)S(1)} all-to-all(f32[16,6,128]{2,1,0:T(8,128)S(1)} %shard_map.65), channel_id=1, replica_groups=mesh['z_lo'=6,'x'=4,'col'=8,'z_hi'=2,'core'=2] {'col','z_hi'}, dimensions={0} | all-to-all | bytes 98304 | tf_op jit(solution)/shard_map/all_to_all | solution.py:30
  159.0 14.5 %all_to_all.46.got_ref = f32[24,4,128]{2,1,0:T(4,128)S(1)} all-to-all(f32[24,4,128]{2,1,0:T(4,128)S(1)} %get-tuple-element.19), channel_id=1, replica_groups=mesh['z_lo'=6,'x'=4,'col'=8,'z_hi'=2,'core'=2] {'z_lo','x'}, dimensions={0} | all-to-all | bytes 98304 | tf_op jit(solution)/shard_map/all_to_all | solution.py:30
  173.5 1.4 shard_map.67
  (4 shorter events, 0.1 us)
Async XLA Ops:
  0.7 0.7 copy-start
  2.7 40.5 %collective-permute-start.1 = (bf16[15,128,128]{2,1,0:T(8,128)(2,1)S(1)}, bf16[15,128,128]{2,1,0:T(8,128)(2,1)S(1)}, u32[]{:S(2)}, u32[]{:S(2)}) collective-permute-start(bf16[15,128,128]{2,1,0:T(8,128)(2,1)S(1)} %and_select_fusion.t0), channel_id=1, source_target_pairs={{0,1},{1,0},{2,3},{3,2},{4,5},{5,4},{6,7},{7,6},{8,9},{9,8},{10,11... | collective-permute-start | bytes 1474568 | tf_op jit(solution)/shard_map/ppermute | solution.py:220
  4.6 24.2 %collective-permute-start = (s32[15]{0:T(128)S(1)}, s32[15]{0:T(128)S(1)}, u32[]{:S(2)}, u32[]{:S(2)}) collective-permute-start(s32[15]{0:T(128)S(1)} %broadcast_select_fusion), channel_id=1, source_target_pairs={{0,1},{1,0},{2,3},{3,2},{4,5},{5,4},{6,7},{7,6},{8,9},{9,8},{10,11... | collective-permute-start | bytes 188 | tf_op jit(solution)/shard_map/ppermute | solution.py:221
  8.3 34.8 %all-to-all-start = ((f32[16,4,128]{2,1,0:T(4,128)}), f32[16,4,128]{2,1,0:T(4,128)S(1)}, u32[]{:S(2)}, u32[]{:S(2)}) async-start(f32[16,4,128]{2,1,0:T(4,128)} %shard_map.59), calls=%async_computation | async-start | bytes 65536 | tf_op jit(solution)/shard_map/all_to_all | solution.py:30

commit v5 on v4

--- a/solution.py
+++ b/solution.py
@@ -30,9 +30,8 @@
     return lax.all_to_all(blocks, axis, 0, 0, tiled=True)
 
 
-def call(body, out_shapes, scalars, arrays, scratch=(), space=pltpu.VMEM, hold=True):
-    if hold:
-        arrays = [pltpu.with_memory_space_constraint(a, pltpu.VMEM) for a in arrays]
+def call(body, out_shapes, scalars, arrays, scratch=(), space=pltpu.VMEM):
+    arrays = [pltpu.with_memory_space_constraint(a, pltpu.VMEM) for a in arrays]
     return pl.pallas_call(
         body,
         out_shape=[space(shape, jnp.float32) for shape in out_shapes],
@@ -50,7 +49,7 @@
 
 def mirror_products(codes, me, x_ref, tile_refs, send_ref):
     rows, vecs = send_ref.shape[0], x_ref.shape[1]
-    slots = tile_refs[0].shape[0]
+    slots = tile_refs[0].shape[0] - 1
     own = x_ref[me]
     for k in range(rows):
         send_ref[k, :vecs, :] = jnp.zeros_like(own)
@@ -70,7 +69,7 @@
 def direct_products(codes, me, got_ref, tile_refs, sums_ref):
     vecs = sums_ref.shape[1]
     rows = got_ref.shape[0]
-    slots = tile_refs[0].shape[0]
+    slots = tile_refs[0].shape[0] - 1
     mirror = got_ref[0, :vecs, :]
     for k in range(1, rows):
         mirror = mirror + got_ref[k, :vecs, :]
@@ -95,18 +94,34 @@
     return total
 
 
-def spread_kernel(vectors_ref, energies_ref, send_ref):
+def prepare_kernel(codes, me, vectors_ref, energies_ref, tiles_ref, send_ref, stored_ref):
     vecs = vectors_ref.shape[0]
+    slots, side = tiles_ref.shape[0], tiles_ref.shape[1]
     energy = jnp.broadcast_to(energies_ref[...], vectors_ref.shape)
     for peer in range(send_ref.shape[0]):
         send_ref[peer, :vecs, :] = vectors_ref[...]
         send_ref[peer, vecs:, :] = energy
-
-
-def start_kernel(codes, me, first_ref, t0, t1, send_ref, base_ref):
+    line = lax.broadcasted_iota(jnp.int32, (side, side), 0)
+    lane = lax.broadcasted_iota(jnp.int32, (side, side), 1)
+    label = jnp.zeros((side, side), jnp.float32)
+    for slot in range(slots):
+        code = codes[slot]
+        bound = jnp.where(code < 0, -side, jnp.where(code == me[2], 0, side))
+        tile = tiles_ref[slot].astype(jnp.float32)
+        stored_ref[slot] = jnp.where(line - lane < bound, tile, 0.0).astype(stored_ref.dtype)
+        label = jnp.where(lane == slot, jnp.maximum(code, 0).astype(jnp.float32), label)
+    stored_ref[slots] = label.astype(stored_ref.dtype)
+
+
+def start_kernel(me, first_ref, t0, t1, send_ref, base_ref, codes):
     cols = base_ref.shape[1]
     halves = first_ref.shape[0] // cols
     vecs = first_ref.shape[1] // 2
+    slots = t0.shape[0] - 1
+    for group, tiles in enumerate((t0, t1)):
+        row = tiles[slots, :1, :].astype(jnp.float32)
+        for slot in range(slots):
+            codes[group * slots + slot] = row[0, slot].astype(jnp.int32)
     for a in range(cols):
         for z in range(halves):
             part = slice(z * vecs, (z + 1) * vecs)
@@ -203,45 +218,42 @@
     row_index = lax.axis_index(ROW)
     col_index = lax.axis_index("col")
     half_index = lax.axis_index("z_hi")
-    side = tiles.shape[1]
+    slots, side = tiles.shape[0], tiles.shape[1]
     vecs = vectors.shape[0]
     wide = vecs * halves
-    present = tile_codes >= 0
-    safe_code = jnp.where(present, tile_codes, 0)
-    on_diagonal = present & (safe_code == col_index * rows + row_index)
-    upper_mask = lax.broadcasted_iota(jnp.int32, (side, side), 1) > lax.broadcasted_iota(
-        jnp.int32, (side, side), 0
-    )
-    keep_mask = present[:, None, None] & (
-        upper_mask[None] | jnp.logical_not(on_diagonal)[:, None, None]
-    )
-    stored = jnp.where(keep_mask, tiles, jnp.zeros((), tiles.dtype))
-    swap = [(0, 1), (1, 0)]
-    near = lax.ppermute(stored, "core", swap)
-    near_code = lax.ppermute(safe_code, "core", swap)
-    codes = jnp.concatenate([safe_code, near_code])
+    me = jnp.stack([col_index, half_index, col_index * rows + row_index]).astype(jnp.int32)
+    first, stored = pl.pallas_call(
+        prepare_kernel,
+        out_shape=[
+            jax.ShapeDtypeStruct((cols * halves, 2 * vecs, side), jnp.float32),
+            pltpu.VMEM((slots + 1, side, side), tiles.dtype),
+        ],
+        in_specs=[SMEM] * 2 + [VMEM] * 3,
+        out_specs=[VMEM] * 2,
+    )(tile_codes, me, vectors, energies[None], tiles)
+    first = exchange(first, COL)
+    near = lax.ppermute(stored, "core", [(0, 1), (1, 0)])
     pair = (stored, near)
-
-    (first,) = call(
-        spread_kernel,
-        [(cols * halves, 2 * vecs, side)],
-        (),
-        (vectors, energies[None]),
-        hold=False,
-    )
-    first = exchange(first, COL)
-    me = jnp.stack([col_index, half_index]).astype(jnp.int32)
 
     row_shape = (rows, 2 * wide, side)
     state_shape = (cols, wide, side)
     col_shape = (cols * halves, cols, wide, side)
+    send, base, codes = pl.pallas_call(
+        start_kernel,
+        out_shape=[
+            pltpu.VMEM(row_shape, jnp.float32),
+            pltpu.VMEM((2, *state_shape), jnp.float32),
+            jax.ShapeDtypeStruct((2 * slots,), jnp.int32),
+        ],
+        in_specs=[SMEM] + [VMEM] * 3,
+        out_specs=[VMEM, VMEM, SMEM],
+    )(me, *(pltpu.with_memory_space_constraint(a, pltpu.VMEM) for a in (first, *pair)))
     scalars = (codes, me)
 
     def col_step(got):
         (send,) = call(direct_kernel, [col_shape], scalars, (got, *pair), [state_shape])
         return exchange(send, COL)
 
-    send, base = call(start_kernel, [row_shape, (2, *state_shape)], scalars, (first, *pair))
     got = col_step(exchange(send, ROW))
     send, x1 = call(second_kernel, [row_shape, state_shape], scalars, (base, got, *pair))
     got = col_step(exchange(send, ROW))

time: 176 us -> 173 us (0.983)
  blocking collectives: 123 us -> 159 us
  starting transfers between devices: 24.2 us -> 1.91 us
  waiting for transfers between devices: 13.7 us -> 0.01 us
  other arithmetic: 2.53 us -> 0.66 us
    all_to_all x7 -> x8, blocking collectives: 123 us -> 159 us  [exchange(): return lax.all_to_all(blocks, axis, 0, 0, tiled=True)]
    all_to_all x1 -> x0, starting transfers between devices: 19.9 us -> none  [exchange(): return lax.all_to_all(blocks, axis, 0, 0, tiled=True)]
    all_to_all x1 -> x0, waiting for transfers between devices: 13.7 us -> none  [exchange(): return lax.all_to_all(blocks, axis, 0, 0, tiled=True)]
    pallas_call x0 -> x2, Pallas kernels: none -> 3.23 us  [the longest x1 1.71 us: on_device(): pl.pallas_call(prepare_kernel, out_shape=[jax.ShapeDtypeStruct((cols * ha...]
    ppermute x2 -> x1, starting transfers between devices: 4.33 us -> 1.91 us  [on_device(): near = lax.ppermute(stored, 'core', [(0, 1), (1, 0)])]
    pallas_call x9 -> x7, Pallas kernels: 9.98 us -> 7.62 us  [call(): pl.pallas_call(body, out_shape=[space(shape, jnp.float32) for shape in ou...]
  transfers between devices with their start and end apart: 3 -> 1, of which waited for: 1 -> 0; matrix products, arithmetic and copies ran while one was open for 1% -> 0% of each run, Pallas kernels for 1% -> 0%
where the time goes in v5:
time: 173 us
  blocking collectives  159 us (92%)
  Pallas kernels  10.8 us (6%)
  starting transfers between devices  1.91 us (1%)
    all_to_all x8, blocking collectives, exchange(): return lax.all_to_all(blocks, axis, 0, 0, tiled=True)  159 us
    pallas_call x7, Pallas kernels, call(): pl.pallas_call(body, out_shape=[space(shape, jnp.float32) for shape in ou...  7.62 us
  transfers between devices with their start and end apart: 1, of which 0 were waited for; matrix products, arithmetic and copies ran while one was open for 0% of the time, Pallas kernels for 0%

profile of v5, /device:TPU:2, one launch (start us, length us, event | category | flops | bytes accessed | tf_op | source)
XLA Modules:
  0.0 172.7 jit_solution(10216388904184590709)
XLA Ops:
  0.6 0.7 pad_add_fusion.me
  1.3 1.7 shard_map.59
  3.0 1.9 %collective-permute-start = (bf16[16,128,128]{2,1,0:T(8,128)(2,1)S(1)}, bf16[16,128,128]{2,1,0:T(8,128)(2,1)S(1)}, u32[]{:S(2)}, u32[]{:S(2)}) collective-permute-start(bf16[16,128,128]{2,1,0:T(8,128)(2,1)S(1)} %get-tuple-element.16.t0), channel_id=1, source_target_pairs={{0,1},{1,0},{2,3},{3,2},{4,5},{5,4},{6,7},{7,6},{8,9},{9,8},{10,11... | collective-permute-start | bytes 1572872 | tf_op jit(solution)/shard_map/ppermute | solution.py:235
  4.9 34.8 %all_to_all.40.first_ref = f32[16,4,128]{2,1,0:T(4,128)S(1)} all-to-all(f32[16,4,128]{2,1,0:T(4,128)} %get-tuple-element.15), channel_id=1, replica_groups=mesh['z_lo'=6,'x'=4,'col'=8,'z_hi'=2,'core'=2] {'col','z_hi'}, dimensions={0} | all-to-all | bytes 65536 | tf_op jit(solution)/shard_map/all_to_all | solution.py:30
  39.8 0.0 collective-permute-done.t1
  39.8 1.5 shard_map.60
  41.3 18.9 %all_to_all.41.got_ref = f32[24,8,128]{2,1,0:T(8,128)S(1)} all-to-all(f32[24,8,128]{2,1,0:T(8,128)S(1)} %get-tuple-element.19), channel_id=1, replica_groups=mesh['z_lo'=6,'x'=4,'col'=8,'z_hi'=2,'core'=2] {'z_lo','x'}, dimensions={0} | all-to-all | bytes 196608 | tf_op jit(solution)/shard_map/all_to_all | solution.py:30
  60.2 1.3 shard_map.61
  61.6 19.3 %all_to_all.42.got_ref = f32[16,8,4,128]{3,2,1,0:T(4,128)S(1)} all-to-all(f32[16,8,4,128]{3,2,1,0:T(4,128)S(1)} %shard_map.61), channel_id=1, replica_groups=mesh['z_lo'=6,'x'=4,'col'=8,'z_hi'=2,'core'=2] {'col','z_hi'}, dimensions={0} | all-to-all | bytes 524288 | tf_op jit(solution)/shard_map/all_to_all | solution.py:30
  80.9 1.1 shard_map.62
  82.0 16.6 %all_to_all.43.got_ref = f32[24,8,128]{2,1,0:T(8,128)S(1)} all-to-all(f32[24,8,128]{2,1,0:T(8,128)S(1)} %get-tuple-element.21), channel_id=1, replica_groups=mesh['z_lo'=6,'x'=4,'col'=8,'z_hi'=2,'core'=2] {'z_lo','x'}, dimensions={0} | all-to-all | bytes 196608 | tf_op jit(solution)/shard_map/all_to_all | solution.py:30
  98.5 1.3 shard_map.63
  99.9 19.7 %all_to_all.44.got_ref = f32[16,8,4,128]{3,2,1,0:T(4,128)S(1)} all-to-all(f32[16,8,4,128]{3,2,1,0:T(4,128)S(1)} %shard_map.63), channel_id=1, replica_groups=mesh['z_lo'=6,'x'=4,'col'=8,'z_hi'=2,'core'=2] {'col','z_hi'}, dimensions={0} | all-to-all | bytes 524288 | tf_op jit(solution)/shard_map/all_to_all | solution.py:30
  119.6 1.1 shard_map.64
  120.7 16.5 %all_to_all.45.got_ref = f32[24,8,128]{2,1,0:T(8,128)S(1)} all-to-all(f32[24,8,128]{2,1,0:T(8,128)S(1)} %get-tuple-element.23), channel_id=1, replica_groups=mesh['z_lo'=6,'x'=4,'col'=8,'z_hi'=2,'core'=2] {'z_lo','x'}, dimensions={0} | all-to-all | bytes 196608 | tf_op jit(solution)/shard_map/all_to_all | solution.py:30
  137.2 1.3 shard_map.65
  138.5 18.6 %all_to_all.46.got_ref = f32[16,6,128]{2,1,0:T(8,128)S(1)} all-to-all(f32[16,6,128]{2,1,0:T(8,128)S(1)} %shard_map.65), channel_id=1, replica_groups=mesh['z_lo'=6,'x'=4,'col'=8,'z_hi'=2,'core'=2] {'col','z_hi'}, dimensions={0} | all-to-all | bytes 98304 | tf_op jit(solution)/shard_map/all_to_all | solution.py:30
  157.1 14.2 %all_to_all.47.got_ref = f32[24,4,128]{2,1,0:T(4,128)S(1)} all-to-all(f32[24,4,128]{2,1,0:T(4,128)S(1)} %get-tuple-element.25), channel_id=1, replica_groups=mesh['z_lo'=6,'x'=4,'col'=8,'z_hi'=2,'core'=2] {'z_lo','x'}, dimensions={0} | all-to-all | bytes 98304 | tf_op jit(solution)/shard_map/all_to_all | solution.py:30
  171.3 1.4 shard_map.67
  (1 shorter events, 0.0 us)
Async XLA Ops:
  3.0 36.7 %collective-permute-start = (bf16[16,128,128]{2,1,0:T(8,128)(2,1)S(1)}, bf16[16,128,128]{2,1,0:T(8,128)(2,1)S(1)}, u32[]{:S(2)}, u32[]{:S(2)}) collective-permute-start(bf16[16,128,128]{2,1,0:T(8,128)(2,1)S(1)} %get-tuple-element.16.t0), channel_id=1, source_target_pairs={{0,1},{1,0},{2,3},{3,2},{4,5},{5,4},{6,7},{7,6},{8,9},{9,8},{10,11... | collective-permute-start | bytes 1572872 | tf_op jit(solution)/shard_map/ppermute | solution.py:235

commit v6 on v5

--- a/solution.py
+++ b/solution.py
@@ -32,6 +32,7 @@
 
 def call(body, out_shapes, scalars, arrays, scratch=(), space=pltpu.VMEM):
     arrays = [pltpu.with_memory_space_constraint(a, pltpu.VMEM) for a in arrays]
+    scalars = [pltpu.with_memory_space_constraint(a, pltpu.SMEM) for a in scalars]
     return pl.pallas_call(
         body,
         out_shape=[space(shape, jnp.float32) for shape in out_shapes],
@@ -94,19 +95,23 @@
     return total
 
 
-def prepare_kernel(codes, me, vectors_ref, energies_ref, tiles_ref, send_ref, stored_ref):
+def prepare_kernel(codes, vectors_ref, energies_ref, tiles_ref, send_ref, stored_ref, me):
     vecs = vectors_ref.shape[0]
     slots, side = tiles_ref.shape[0], tiles_ref.shape[1]
     energy = jnp.broadcast_to(energies_ref[...], vectors_ref.shape)
     for peer in range(send_ref.shape[0]):
         send_ref[peer, :vecs, :] = vectors_ref[...]
         send_ref[peer, vecs:, :] = energy
+    col_index = lax.axis_index("col")
+    me[0] = col_index
+    me[1] = lax.axis_index("z_hi")
+    diagonal = col_index * lax.axis_size(ROW) + lax.axis_index(ROW)
     line = lax.broadcasted_iota(jnp.int32, (side, side), 0)
     lane = lax.broadcasted_iota(jnp.int32, (side, side), 1)
     label = jnp.zeros((side, side), jnp.float32)
     for slot in range(slots):
         code = codes[slot]
-        bound = jnp.where(code < 0, -side, jnp.where(code == me[2], 0, side))
+        bound = jnp.where(code < 0, -side, jnp.where(code == diagonal, 0, side))
         tile = tiles_ref[slot].astype(jnp.float32)
         stored_ref[slot] = jnp.where(line - lane < bound, tile, 0.0).astype(stored_ref.dtype)
         label = jnp.where(lane == slot, jnp.maximum(code, 0).astype(jnp.float32), label)
@@ -215,22 +220,19 @@
     rows = lax.axis_size(ROW)
     cols = lax.axis_size("col")
     halves = lax.axis_size("z_hi")
-    row_index = lax.axis_index(ROW)
-    col_index = lax.axis_index("col")
-    half_index = lax.axis_index("z_hi")
     slots, side = tiles.shape[0], tiles.shape[1]
     vecs = vectors.shape[0]
     wide = vecs * halves
-    me = jnp.stack([col_index, half_index, col_index * rows + row_index]).astype(jnp.int32)
-    first, stored = pl.pallas_call(
+    first, stored, me = pl.pallas_call(
         prepare_kernel,
         out_shape=[
             jax.ShapeDtypeStruct((cols * halves, 2 * vecs, side), jnp.float32),
             pltpu.VMEM((slots + 1, side, side), tiles.dtype),
+            pltpu.SMEM((2,), jnp.int32),
         ],
-        in_specs=[SMEM] * 2 + [VMEM] * 3,
-        out_specs=[VMEM] * 2,
-    )(tile_codes, me, vectors, energies[None], tiles)
+        in_specs=[SMEM] + [VMEM] * 3,
+        out_specs=[VMEM, VMEM, SMEM],
+    )(tile_codes, vectors, energies[None], tiles)
     first = exchange(first, COL)
     near = lax.ppermute(stored, "core", [(0, 1), (1, 0)])
     pair = (stored, near)
@@ -243,11 +245,14 @@
         out_shape=[
             pltpu.VMEM(row_shape, jnp.float32),
             pltpu.VMEM((2, *state_shape), jnp.float32),
-            jax.ShapeDtypeStruct((2 * slots,), jnp.int32),
+            pltpu.SMEM((2 * slots,), jnp.int32),
         ],
         in_specs=[SMEM] + [VMEM] * 3,
         out_specs=[VMEM, VMEM, SMEM],
-    )(me, *(pltpu.with_memory_space_constraint(a, pltpu.VMEM) for a in (first, *pair)))
+    )(
+        pltpu.with_memory_space_constraint(me, pltpu.SMEM),
+        *(pltpu.with_memory_space_constraint(a, pltpu.VMEM) for a in (first, *pair)),
+    )
     scalars = (codes, me)
 
     def col_step(got):

time: 173 us -> 167 us (0.965)
  Pallas kernels: 10.8 us -> 5.83 us
    pallas_call x7, Pallas kernels: 7.62 us -> 3.6 us  [call(): pl.pallas_call(body, out_shape=[space(shape, jnp.float32) for shape in ou...]
where the time goes in v6:
time: 167 us
  blocking collectives  159 us (95%)
  Pallas kernels  5.83 us (3%)
  starting transfers between devices  1.91 us (1%)
    all_to_all x8, blocking collectives, exchange(): return lax.all_to_all(blocks, axis, 0, 0, tiled=True)  159 us
    pallas_call x7, Pallas kernels, call(): pl.pallas_call(body, out_shape=[space(shape, jnp.float32) for shape in ou...  3.6 us
  transfers between devices with their start and end apart: 1, of which 0 were waited for; matrix products, arithmetic and copies ran while one was open for 0% of the time, Pallas kernels for 0%

profile of v6, /device:TPU:2, one launch (start us, length us, event | category | flops | bytes accessed | tf_op | source)
XLA Modules:
  0.0 167.0 jit_solution(13685868398161154167)
XLA Ops:
  0.6 1.7 %shard_map.59 = (f32[16,4,128]{2,1,0:T(4,128)}, bf16[16,128,128]{2,1,0:T(8,128)(2,1)S(1)}, s32[2]{0:T(128)S(4)}) custom-call(s32[15]{0:T(128)} %codes.1, f32[2,128]{1,0:T(2,128)} %vectors_ref.1, f32[1,128]{1,0:T(1,128)} %bitcast.2, bf16[15,128,128]{2,1,0:T(8,128)(2,1)} %tiles_ref.1), custom_call_target="tpu_custom_call" | custom-call | tf_op jit(solution)/shard_map/pallas_call | solution.py:226
  2.3 1.9 %collective-permute-start = (bf16[16,128,128]{2,1,0:T(8,128)(2,1)S(1)}, bf16[16,128,128]{2,1,0:T(8,128)(2,1)S(1)}, u32[]{:S(2)}, u32[]{:S(2)}) collective-permute-start(bf16[16,128,128]{2,1,0:T(8,128)(2,1)S(1)} %get-tuple-element.18.t0), channel_id=1, source_target_pairs={{0,1},{1,0},{2,3},{3,2},{4,5},{5,4},{6,7},{7,6},{8,9},{9,8},{10,11... | collective-permute-start | bytes 1572872 | tf_op jit(solution)/shard_map/ppermute | solution.py:237
  4.3 34.8 %all_to_all.40.first_ref = f32[16,4,128]{2,1,0:T(4,128)S(1)} all-to-all(f32[16,4,128]{2,1,0:T(4,128)} %get-tuple-element.17), channel_id=1, replica_groups=mesh['z_lo'=6,'x'=4,'col'=8,'z_hi'=2,'core'=2] {'col','z_hi'}, dimensions={0} | all-to-all | bytes 65536 | tf_op jit(solution)/shard_map/all_to_all | solution.py:30
  39.1 0.0 collective-permute-done.t1
  39.1 0.5 shard_map.60
  39.6 18.9 %all_to_all.41.got_ref = f32[24,8,128]{2,1,0:T(8,128)S(1)} all-to-all(f32[24,8,128]{2,1,0:T(8,128)S(1)} %get-tuple-element.21), channel_id=1, replica_groups=mesh['z_lo'=6,'x'=4,'col'=8,'z_hi'=2,'core'=2] {'z_lo','x'}, dimensions={0} | all-to-all | bytes 196608 | tf_op jit(solution)/shard_map/all_to_all | solution.py:30
  58.5 0.7 shard_map.61
  59.2 19.3 %all_to_all.42.got_ref = f32[16,8,4,128]{3,2,1,0:T(4,128)S(1)} all-to-all(f32[16,8,4,128]{3,2,1,0:T(4,128)S(1)} %shard_map.61), channel_id=1, replica_groups=mesh['z_lo'=6,'x'=4,'col'=8,'z_hi'=2,'core'=2] {'col','z_hi'}, dimensions={0} | all-to-all | bytes 524288 | tf_op jit(solution)/shard_map/all_to_all | solution.py:30
  78.5 0.4 shard_map.62
  78.9 16.6 %all_to_all.43.got_ref = f32[24,8,128]{2,1,0:T(8,128)S(1)} all-to-all(f32[24,8,128]{2,1,0:T(8,128)S(1)} %get-tuple-element.23), channel_id=1, replica_groups=mesh['z_lo'=6,'x'=4,'col'=8,'z_hi'=2,'core'=2] {'z_lo','x'}, dimensions={0} | all-to-all | bytes 196608 | tf_op jit(solution)/shard_map/all_to_all | solution.py:30
  95.5 0.7 shard_map.63
  96.2 19.7 %all_to_all.44.got_ref = f32[16,8,4,128]{3,2,1,0:T(4,128)S(1)} all-to-all(f32[16,8,4,128]{3,2,1,0:T(4,128)S(1)} %shard_map.63), channel_id=1, replica_groups=mesh['z_lo'=6,'x'=4,'col'=8,'z_hi'=2,'core'=2] {'col','z_hi'}, dimensions={0} | all-to-all | bytes 524288 | tf_op jit(solution)/shard_map/all_to_all | solution.py:30
  115.9 0.4 shard_map.64
  116.3 16.5 %all_to_all.45.got_ref = f32[24,8,128]{2,1,0:T(8,128)S(1)} all-to-all(f32[24,8,128]{2,1,0:T(8,128)S(1)} %get-tuple-element.25), channel_id=1, replica_groups=mesh['z_lo'=6,'x'=4,'col'=8,'z_hi'=2,'core'=2] {'z_lo','x'}, dimensions={0} | all-to-all | bytes 196608 | tf_op jit(solution)/shard_map/all_to_all | solution.py:30
  132.8 0.7 shard_map.65
  133.5 18.6 %all_to_all.46.got_ref = f32[16,6,128]{2,1,0:T(8,128)S(1)} all-to-all(f32[16,6,128]{2,1,0:T(8,128)S(1)} %shard_map.65), channel_id=1, replica_groups=mesh['z_lo'=6,'x'=4,'col'=8,'z_hi'=2,'core'=2] {'col','z_hi'}, dimensions={0} | all-to-all | bytes 98304 | tf_op jit(solution)/shard_map/all_to_all | solution.py:30
  152.1 14.2 %all_to_all.47.got_ref = f32[24,4,128]{2,1,0:T(4,128)S(1)} all-to-all(f32[24,4,128]{2,1,0:T(4,128)S(1)} %get-tuple-element.27), channel_id=1, replica_groups=mesh['z_lo'=6,'x'=4,'col'=8,'z_hi'=2,'core'=2] {'z_lo','x'}, dimensions={0} | all-to-all | bytes 98304 | tf_op jit(solution)/shard_map/all_to_all | solution.py:30
  166.2 0.8 shard_map.67
  (1 shorter events, 0.0 us)
Async XLA Ops:
  2.3 36.7 %collective-permute-start = (bf16[16,128,128]{2,1,0:T(8,128)(2,1)S(1)}, bf16[16,128,128]{2,1,0:T(8,128)(2,1)S(1)}, u32[]{:S(2)}, u32[]{:S(2)}) collective-permute-start(bf16[16,128,128]{2,1,0:T(8,128)(2,1)S(1)} %get-tuple-element.18.t0), channel_id=1, source_target_pairs={{0,1},{1,0},{2,3},{3,2},{4,5},{5,4},{6,7},{7,6},{8,9},{9,8},{10,11... | collective-permute-start | bytes 1572872 | tf_op jit(solution)/shard_map/ppermute | solution.py:237

commit v7 on v6

--- a/solution.py
+++ b/solution.py
@@ -7,7 +7,7 @@
 from jax.sharding import PartitionSpec as P
 
 ROW = ("z_lo", "x")
-COL = ("col", "z_hi")
+COL = "col"
 REP = ("z_hi", "core")
 ROW_COL = ("z_lo", "x", "col")
 ROW_COL_REP = ("z_lo", "x", "col", "z_hi", "core")
@@ -118,12 +118,12 @@
     stored_ref[slots] = label.astype(stored_ref.dtype)
 
 
-def start_kernel(me, first_ref, t0, t1, send_ref, base_ref, codes):
+def start_kernel(me, first_ref, t0, t1, t2, t3, send_ref, base_ref, codes):
     cols = base_ref.shape[1]
     halves = first_ref.shape[0] // cols
     vecs = first_ref.shape[1] // 2
     slots = t0.shape[0] - 1
-    for group, tiles in enumerate((t0, t1)):
+    for group, tiles in enumerate((t0, t1, t2, t3)):
         row = tiles[slots, :1, :].astype(jnp.float32)
         for slot in range(slots):
             codes[group * slots + slot] = row[0, slot].astype(jnp.int32)
@@ -132,35 +132,35 @@
             part = slice(z * vecs, (z + 1) * vecs)
             base_ref[0, a, part, :] = first_ref[a * halves + z, :vecs, :]
             base_ref[1, a, part, :] = first_ref[a * halves + z, vecs:, :]
-    mirror_products(codes, me[0], base_ref.at[0], (t0, t1), send_ref)
-
-
-def second_kernel(codes, me, base_ref, got_ref, t0, t1, send_ref, x_ref):
+    mirror_products(codes, me[0], base_ref.at[0], (t0, t1, t2, t3), send_ref)
+
+
+def second_kernel(codes, me, base_ref, got_ref, t0, t1, t2, t3, send_ref, x_ref):
     for a in range(x_ref.shape[0]):
         x = base_ref[0, a]
         image = base_ref[1, a] * x + summed(got_ref, a)
         x_ref[a] = (image - centre * x) * (sigma_first / half)
-    mirror_products(codes, me[0], x_ref, (t0, t1), send_ref)
-
-
-def third_kernel(codes, me, base_ref, last_ref, got_ref, t0, t1, send_ref, x_ref):
+    mirror_products(codes, me[0], x_ref, (t0, t1, t2, t3), send_ref)
+
+
+def third_kernel(codes, me, base_ref, last_ref, got_ref, t0, t1, t2, t3, send_ref, x_ref):
     for a in range(x_ref.shape[0]):
         x = last_ref[a]
         image = base_ref[1, a] * x + summed(got_ref, a)
         x_ref[a] = (image - centre * x) * (2.0 * sigma_next / half) - (
             sigma_first * sigma_next
         ) * base_ref[0, a]
-    mirror_products(codes, me[0], x_ref, (t0, t1), send_ref)
-
-
-def direct_kernel(codes, me, got_ref, t0, t1, send_ref, sums_ref):
-    direct_products(codes, me[0], got_ref, (t0, t1), sums_ref)
+    mirror_products(codes, me[0], x_ref, (t0, t1, t2, t3), send_ref)
+
+
+def direct_kernel(codes, me, got_ref, t0, t1, t2, t3, send_ref, sums_ref):
+    direct_products(codes, me[0], got_ref, (t0, t1, t2, t3), sums_ref)
     for peer in range(send_ref.shape[0]):
         send_ref[peer] = sums_ref[...]
 
 
-def last_direct_kernel(codes, me, base_ref, x_ref, got_ref, t0, t1, send_ref, sums_ref):
-    direct_products(codes, me[0], got_ref, (t0, t1), sums_ref)
+def last_direct_kernel(codes, me, base_ref, x_ref, got_ref, t0, t1, t2, t3, send_ref, sums_ref):
+    direct_products(codes, me[0], got_ref, (t0, t1, t2, t3), sums_ref)
     cols, vecs = sums_ref.shape[0], send_ref.shape[1] // 3
     halves = send_ref.shape[0] // cols
     x = x_ref[me[0]]
@@ -170,8 +170,7 @@
         crossed = crossed + x_ref[a] * sums_ref[a]
     for z in range(halves):
         part = slice(z * vecs, (z + 1) * vecs)
-        once = jnp.where(me[1] == z, 1.0, 0.0)
-        square = x[part] * x[part] * once
+        square = x[part] * x[part]
         local = crossed[part] + energy[part] * square
         for c in range(cols):
             send_ref[c * halves + z, :vecs, :] = sums_ref[c, part, :]
@@ -219,7 +218,7 @@
 def on_device(vectors, energies, tiles, tile_codes):
     rows = lax.axis_size(ROW)
     cols = lax.axis_size("col")
-    halves = lax.axis_size("z_hi")
+    halves = 1
     slots, side = tiles.shape[0], tiles.shape[1]
     vecs = vectors.shape[0]
     wide = vecs * halves
@@ -234,8 +233,12 @@
         out_specs=[VMEM, VMEM, SMEM],
     )(tile_codes, vectors, energies[None], tiles)
     first = exchange(first, COL)
-    near = lax.ppermute(stored, "core", [(0, 1), (1, 0)])
-    pair = (stored, near)
+    swap = [(0, 1), (1, 0)]
+    far = lax.ppermute(stored, "z_hi", swap)
+    near = lax.ppermute(stored, "core", swap)
+    far, _ = lax.optimization_barrier((far, first))
+    far_near = lax.ppermute(far, "core", swap)
+    pair = (stored, near, far, far_near)
 
     row_shape = (rows, 2 * wide, side)
     state_shape = (cols, wide, side)
@@ -245,9 +248,9 @@
         out_shape=[
             pltpu.VMEM(row_shape, jnp.float32),
             pltpu.VMEM((2, *state_shape), jnp.float32),
-            pltpu.SMEM((2 * slots,), jnp.int32),
+            pltpu.SMEM((len(pair) * slots,), jnp.int32),
         ],
-        in_specs=[SMEM] + [VMEM] * 3,
+        in_specs=[SMEM] + [VMEM] * (1 + len(pair)),
         out_specs=[VMEM, VMEM, SMEM],
     )(
         pltpu.with_memory_space_constraint(me, pltpu.SMEM),

time: 167 us -> 160 us (0.958)
  blocking collectives: 159 us -> 117 us
  starting transfers between devices: 1.91 us -> 26.1 us
  waiting for transfers between devices: 0.01 us -> 7.73 us
  Pallas kernels: 5.83 us -> 8.2 us
    all_to_all x8 -> x7, blocking collectives: 159 us -> 117 us  [exchange(): return lax.all_to_all(blocks, axis, 0, 0, tiled=True)]
    ppermute x1 -> x3, starting transfers between devices: 1.91 us -> 18.9 us  [the longest x1 15.1 us: on_device(): far = lax.ppermute(stored, 'z_hi', swap)]
    all_to_all x0 -> x1, starting transfers between devices: none -> 7.11 us  [exchange(): return lax.all_to_all(blocks, axis, 0, 0, tiled=True)]
    all_to_all x0 -> x1, waiting for transfers between devices: none -> 5.86 us  [exchange(): return lax.all_to_all(blocks, axis, 0, 0, tiled=True)]
    pallas_call x7, Pallas kernels: 3.6 us -> 5.65 us  [call(): pl.pallas_call(body, out_shape=[space(shape, jnp.float32) for shape in ou...]
    ppermute x1 -> x3, waiting for transfers between devices: 0.01 us -> 1.87 us  [the longest x1 1.87 us: on_device(): far_near = lax.ppermute(far, 'core', swap)]
  transfers between devices with their start and end apart: 1 -> 4, of which waited for: 0 -> 2; matrix products, arithmetic and copies ran while one was open for 0% -> 0% of each run, Pallas kernels for 0% -> 0%
where the time goes in v7:
time: 160 us; the launch traced here: 159 us
  blocking collectives  117 us (73%)
  starting transfers between devices  26.1 us (16%)
  Pallas kernels  8.2 us (5%)
  waiting for transfers between devices  7.73 us (5%)
    all_to_all x7, blocking collectives, exchange(): return lax.all_to_all(blocks, axis, 0, 0, tiled=True)  117 us
    ppermute x1, starting transfers between devices, on_device(): far = lax.ppermute(stored, 'z_hi', swap)  15.1 us
    all_to_all x1, starting transfers between devices, exchange(): return lax.all_to_all(blocks, axis, 0, 0, tiled=True)  7.11 us
    all_to_all x1, waiting for transfers between devices, exchange(): return lax.all_to_all(blocks, axis, 0, 0, tiled=True)  5.86 us
    pallas_call x7, Pallas kernels, call(): pl.pallas_call(body, out_shape=[space(shape, jnp.float32) for shape in ou...  5.65 us
  transfers between devices with their start and end apart: 4, of which 2 were waited for; matrix products, arithmetic and copies ran while one was open for 0% of the time, Pallas kernels for 0%

profile of v7, /device:TPU:2, one launch (start us, length us, event | category | flops | bytes accessed | tf_op | source)
XLA Modules:
  0.0 159.5 jit_solution(7488519244035134223)
XLA Ops:
  0.6 1.7 %shard_map.59 = (f32[8,4,128]{2,1,0:T(4,128)}, bf16[16,128,128]{2,1,0:T(8,128)(2,1)S(1)}, s32[2]{0:T(128)S(4)}) custom-call(s32[15]{0:T(128)} %codes.1, f32[2,128]{1,0:T(2,128)} %vectors_ref.1, f32[1,128]{1,0:T(1,128)} %bitcast.2, bf16[15,128,128]{2,1,0:T(8,128)(2,1)} %tiles_ref.1), custom_call_target="tpu_custom_call" | custom-call | tf_op jit(solution)/shard_map/pallas_call | solution.py:225
  2.3 15.1 %collective-permute-start.1 = (bf16[16,128,128]{2,1,0:T(8,128)(2,1)S(1)}, bf16[16,128,128]{2,1,0:T(8,128)(2,1)S(1)}, u32[]{:S(2)}, u32[]{:S(2)}) collective-permute-start(bf16[16,128,128]{2,1,0:T(8,128)(2,1)S(1)} %get-tuple-element.19.t0), channel_id=1, source_target_pairs={{0,2},{2,0},{1,3},{3,1},{4,6},{6,4},{5,7},{7,5},{8,10},{10,8},{9,1... | collective-permute-start | bytes 1572872 | tf_op jit(solution)/shard_map/ppermute | solution.py:237
  17.5 7.1 %all-to-all-start = ((f32[8,4,128]{2,1,0:T(4,128)}), f32[8,4,128]{2,1,0:T(4,128)S(1)}, u32[]{:S(2)}, u32[]{:S(2)}) async-start(f32[8,4,128]{2,1,0:T(4,128)} %get-tuple-element.18), calls=%async_computation | async-start | bytes 32768 | tf_op jit(solution)/shard_map/all_to_all | solution.py:30
  24.6 1.9 %collective-permute-start = (bf16[16,128,128]{2,1,0:T(8,128)(2,1)S(1)}, bf16[16,128,128]{2,1,0:T(8,128)(2,1)S(1)}, u32[]{:S(2)}, u32[]{:S(2)}) collective-permute-start(bf16[16,128,128]{2,1,0:T(8,128)(2,1)S(1)} %get-tuple-element.19.t0), channel_id=1, source_target_pairs={{0,1},{1,0},{2,3},{3,2},{4,5},{5,4},{6,7},{7,6},{8,9},{9,8},{10,11... | collective-permute-start | bytes 1572872 | tf_op jit(solution)/shard_map/ppermute | solution.py:238
  26.5 5.9 %all-to-all-done.first_ref = f32[8,4,128]{2,1,0:T(4,128)S(1)} async-done(((f32[8,4,128]{2,1,0:T(4,128)}), f32[8,4,128]{2,1,0:T(4,128)S(1)}, u32[]{:S(2)}, u32[]{:S(2)}) %all-to-all-start) | async-done | bytes 16416 | tf_op jit(solution)/shard_map/all_to_all | solution.py:30
  32.4 0.0 collective-permute-done.1.t2
  32.4 1.9 %collective-permute-start.2 = (bf16[16,128,128]{2,1,0:T(8,128)(2,1)S(1)}, bf16[16,128,128]{2,1,0:T(8,128)(2,1)S(1)}, u32[]{:S(2)}, u32[]{:S(2)}) collective-permute-start(bf16[16,128,128]{2,1,0:T(8,128)(2,1)S(1)} %collective-permute-done.1.t2), channel_id=1, source_target_pairs={{0,1},{1,0},{2,3},{3,2},{4,5},{5,4},{6,7},{7,6},{8,9},{9,8},{10,11... | collective-permute-start | bytes 1572872 | tf_op jit(solution)/shard_map/ppermute | solution.py:240
  34.3 0.0 collective-permute-done.t1
  34.3 1.9 %collective-permute-done.2.t3 = bf16[16,128,128]{2,1,0:T(8,128)(2,1)S(1)} collective-permute-done((bf16[16,128,128]{2,1,0:T(8,128)(2,1)S(1)}, bf16[16,128,128]{2,1,0:T(8,128)(2,1)S(1)}, u32[]{:S(2)}, u32[]{:S(2)}) %collective-permute-start.2) | collective-permute-done | bytes 524320 | tf_op jit(solution)/shard_map/ppermute | solution.py:240
  36.1 0.9 shard_map.60
  37.0 38.3 %all_to_all.40.got_ref = f32[24,4,128]{2,1,0:T(4,128)S(1)} all-to-all(f32[24,4,128]{2,1,0:T(4,128)S(1)} %get-tuple-element.23), channel_id=1, replica_groups=mesh['z_lo'=6,'x'=4,'col'=8,'z_hi'=2,'core'=2] {'z_lo','x'}, dimensions={0} | all-to-all | bytes 98304 | tf_op jit(solution)/shard_map/all_to_all | solution.py:30
  75.3 1.2 shard_map.61
  76.5 15.3 %all_to_all.41.got_ref = f32[8,8,2,128]{3,2,1,0:T(2,128)S(1)} all-to-all(f32[8,8,2,128]{3,2,1,0:T(2,128)S(1)} %shard_map.61), channel_id=1, replica_groups=mesh['z_lo'=6,'x'=4,'col'=8,'z_hi'=2,'core'=2] {'col'}, dimensions={0} | all-to-all | bytes 131072 | tf_op jit(solution)/shard_map/all_to_all | solution.py:30
  91.7 0.7 shard_map.62
  92.4 14.1 %all_to_all.42.got_ref = f32[24,4,128]{2,1,0:T(4,128)S(1)} all-to-all(f32[24,4,128]{2,1,0:T(4,128)S(1)} %get-tuple-element.25), channel_id=1, replica_groups=mesh['z_lo'=6,'x'=4,'col'=8,'z_hi'=2,'core'=2] {'z_lo','x'}, dimensions={0} | all-to-all | bytes 98304 | tf_op jit(solution)/shard_map/all_to_all | solution.py:30
  106.4 1.2 shard_map.63
  107.6 10.8 %all_to_all.43.got_ref = f32[8,8,2,128]{3,2,1,0:T(2,128)S(1)} all-to-all(f32[8,8,2,128]{3,2,1,0:T(2,128)S(1)} %shard_map.63), channel_id=1, replica_groups=mesh['z_lo'=6,'x'=4,'col'=8,'z_hi'=2,'core'=2] {'col'}, dimensions={0} | all-to-all | bytes 131072 | tf_op jit(solution)/shard_map/all_to_all | solution.py:30
  118.4 0.7 shard_map.64
  119.1 14.1 %all_to_all.44.got_ref = f32[24,4,128]{2,1,0:T(4,128)S(1)} all-to-all(f32[24,4,128]{2,1,0:T(4,128)S(1)} %get-tuple-element.27), channel_id=1, replica_groups=mesh['z_lo'=6,'x'=4,'col'=8,'z_hi'=2,'core'=2] {'z_lo','x'}, dimensions={0} | all-to-all | bytes 98304 | tf_op jit(solution)/shard_map/all_to_all | solution.py:30
  133.1 1.2 shard_map.65
  134.3 10.4 %all_to_all.45.got_ref = f32[8,6,128]{2,1,0:T(8,128)S(1)} all-to-all(f32[8,6,128]{2,1,0:T(8,128)S(1)} %shard_map.65), channel_id=1, replica_groups=mesh['z_lo'=6,'x'=4,'col'=8,'z_hi'=2,'core'=2] {'col'}, dimensions={0} | all-to-all | bytes 49152 | tf_op jit(solution)/shard_map/all_to_all | solution.py:30
  144.7 14.0 %all_to_all.46.got_ref = f32[24,4,128]{2,1,0:T(4,128)S(1)} all-to-all(f32[24,4,128]{2,1,0:T(4,128)S(1)} %get-tuple-element.29), channel_id=1, replica_groups=mesh['z_lo'=6,'x'=4,'col'=8,'z_hi'=2,'core'=2] {'z_lo','x'}, dimensions={0} | all-to-all | bytes 98304 | tf_op jit(solution)/shard_map/all_to_all | solution.py:30
  158.7 0.8 shard_map.67
  (1 shorter events, 0.0 us)
Async XLA Ops:
  2.3 30.0 %collective-permute-start.1 = (bf16[16,128,128]{2,1,0:T(8,128)(2,1)S(1)}, bf16[16,128,128]{2,1,0:T(8,128)(2,1)S(1)}, u32[]{:S(2)}, u32[]{:S(2)}) collective-permute-start(bf16[16,128,128]{2,1,0:T(8,128)(2,1)S(1)} %get-tuple-element.19.t0), channel_id=1, source_target_pairs={{0,2},{2,0},{1,3},{3,1},{4,6},{6,4},{5,7},{7,5},{8,10},{10,8},{9,1... | collective-permute-start | bytes 1572872 | tf_op jit(solution)/shard_map/ppermute | solution.py:237
  17.5 14.9 %all-to-all-start = ((f32[8,4,128]{2,1,0:T(4,128)}), f32[8,4,128]{2,1,0:T(4,128)S(1)}, u32[]{:S(2)}, u32[]{:S(2)}) async-start(f32[8,4,128]{2,1,0:T(4,128)} %get-tuple-element.18), calls=%async_computation | async-start | bytes 32768 | tf_op jit(solution)/shard_map/all_to_all | solution.py:30
  24.6 9.7 %collective-permute-start = (bf16[16,128,128]{2,1,0:T(8,128)(2,1)S(1)}, bf16[16,128,128]{2,1,0:T(8,128)(2,1)S(1)}, u32[]{:S(2)}, u32[]{:S(2)}) collective-permute-start(bf16[16,128,128]{2,1,0:T(8,128)(2,1)S(1)} %get-tuple-element.19.t0), channel_id=1, source_target_pairs={{0,1},{1,0},{2,3},{3,2},{4,5},{5,4},{6,7},{7,6},{8,9},{9,8},{10,11... | collective-permute-start | bytes 1572872 | tf_op jit(solution)/shard_map/ppermute | solution.py:238
  32.4 3.8 %collective-permute-start.2 = (bf16[16,128,128]{2,1,0:T(8,128)(2,1)S(1)}, bf16[16,128,128]{2,1,0:T(8,128)(2,1)S(1)}, u32[]{:S(2)}, u32[]{:S(2)}) collective-permute-start(bf16[16,128,128]{2,1,0:T(8,128)(2,1)S(1)} %collective-permute-done.1.t2), channel_id=1, source_target_pairs={{0,1},{1,0},{2,3},{3,2},{4,5},{5,4},{6,7},{7,6},{8,9},{9,8},{10,11... | collective-permute-start | bytes 1572872 | tf_op jit(solution)/shard_map/ppermute | solution.py:240

commit v8 on v7

--- a/solution.py
+++ b/solution.py
@@ -24,6 +24,7 @@
 
 VMEM = pl.BlockSpec(memory_space=pltpu.VMEM)
 SMEM = pl.BlockSpec(memory_space=pltpu.SMEM)
+LABEL_ROWS = 16
 
 
 def exchange(blocks, axis):
@@ -48,44 +49,49 @@
     return a, code - a * rows
 
 
+def slots_of(tile_refs):
+    place_in_list = 0
+    for tiles in tile_refs:
+        side = tiles.shape[1]
+        for slot in range(tiles.shape[0] // side):
+            yield place_in_list, tiles.at[slot * side : (slot + 1) * side, :]
+            place_in_list += 1
+
+
 def mirror_products(codes, me, x_ref, tile_refs, send_ref):
     rows, vecs = send_ref.shape[0], x_ref.shape[1]
-    slots = tile_refs[0].shape[0] - 1
     own = x_ref[me]
     for k in range(rows):
         send_ref[k, :vecs, :] = jnp.zeros_like(own)
         send_ref[k, vecs:, :] = own
-    for group, tiles in enumerate(tile_refs):
-        for slot in range(slots):
-            a, k = place(codes[group * slots + slot], rows)
-            part = lax.dot_general(
-                x_ref[a].astype(jnp.bfloat16),
-                tiles[slot],
-                (((1,), (0,)), ((), ())),
-                preferred_element_type=jnp.float32,
-            )
-            send_ref[k, :vecs, :] += part
+    for slot, tile in slots_of(tile_refs):
+        a, k = place(codes[slot], rows)
+        part = lax.dot_general(
+            x_ref[a].astype(jnp.bfloat16),
+            tile[...],
+            (((1,), (0,)), ((), ())),
+            preferred_element_type=jnp.float32,
+        )
+        send_ref[k, :vecs, :] += part
 
 
 def direct_products(codes, me, got_ref, tile_refs, sums_ref):
     vecs = sums_ref.shape[1]
     rows = got_ref.shape[0]
-    slots = tile_refs[0].shape[0] - 1
     mirror = got_ref[0, :vecs, :]
     for k in range(1, rows):
         mirror = mirror + got_ref[k, :vecs, :]
     sums_ref[...] = jnp.zeros_like(sums_ref)
     sums_ref[me] = mirror
-    for group, tiles in enumerate(tile_refs):
-        for slot in range(slots):
-            a, k = place(codes[group * slots + slot], rows)
-            part = lax.dot_general(
-                got_ref[k, vecs:, :].astype(jnp.bfloat16),
-                tiles[slot],
-                (((1,), (1,)), ((), ())),
-                preferred_element_type=jnp.float32,
-            )
-            sums_ref[a] += part
+    for slot, tile in slots_of(tile_refs):
+        a, k = place(codes[slot], rows)
+        part = lax.dot_general(
+            got_ref[k, vecs:, :].astype(jnp.bfloat16),
+            tile[...],
+            (((1,), (1,)), ((), ())),
+            preferred_element_type=jnp.float32,
+        )
+        sums_ref[a] += part
 
 
 def summed(got_ref, a):
@@ -95,72 +101,85 @@
     return total
 
 
-def prepare_kernel(codes, vectors_ref, energies_ref, tiles_ref, send_ref, stored_ref, me):
+def prepare_kernel(codes, vectors_ref, energies_ref, tiles_ref, send_ref, *refs):
+    *part_refs, me = refs
     vecs = vectors_ref.shape[0]
-    slots, side = tiles_ref.shape[0], tiles_ref.shape[1]
+    side = tiles_ref.shape[1]
     energy = jnp.broadcast_to(energies_ref[...], vectors_ref.shape)
     for peer in range(send_ref.shape[0]):
         send_ref[peer, :vecs, :] = vectors_ref[...]
         send_ref[peer, vecs:, :] = energy
     col_index = lax.axis_index("col")
     me[0] = col_index
-    me[1] = lax.axis_index("z_hi")
     diagonal = col_index * lax.axis_size(ROW) + lax.axis_index(ROW)
     line = lax.broadcasted_iota(jnp.int32, (side, side), 0)
     lane = lax.broadcasted_iota(jnp.int32, (side, side), 1)
-    label = jnp.zeros((side, side), jnp.float32)
-    for slot in range(slots):
+    last = part_refs[-1]
+    label_rows = last.shape[0] % side
+    label_lane = lax.broadcasted_iota(jnp.int32, (label_rows, side), 1)
+    label = jnp.zeros((label_rows, side), jnp.float32)
+    for slot, stored in slots_of(part_refs):
         code = codes[slot]
         bound = jnp.where(code < 0, -side, jnp.where(code == diagonal, 0, side))
         tile = tiles_ref[slot].astype(jnp.float32)
-        stored_ref[slot] = jnp.where(line - lane < bound, tile, 0.0).astype(stored_ref.dtype)
-        label = jnp.where(lane == slot, jnp.maximum(code, 0).astype(jnp.float32), label)
-    stored_ref[slots] = label.astype(stored_ref.dtype)
-
-
-def start_kernel(me, first_ref, t0, t1, t2, t3, send_ref, base_ref, codes):
+        stored[...] = jnp.where(line - lane < bound, tile, 0.0).astype(last.dtype)
+        label = jnp.where(label_lane == slot, jnp.maximum(code, 0).astype(jnp.float32), label)
+    last[last.shape[0] - label_rows :, :] = label.astype(last.dtype)
+
+
+def start_kernel(me, first_ref, *refs):
+    *tile_refs, send_ref, base_ref, codes = refs
     cols = base_ref.shape[1]
     halves = first_ref.shape[0] // cols
     vecs = first_ref.shape[1] // 2
-    slots = t0.shape[0] - 1
-    for group, tiles in enumerate((t0, t1, t2, t3)):
-        row = tiles[slots, :1, :].astype(jnp.float32)
-        for slot in range(slots):
-            codes[group * slots + slot] = row[0, slot].astype(jnp.int32)
+    side = first_ref.shape[2]
+    place_in_list = slots = 0
+    for tiles in tile_refs:
+        slots += tiles.shape[0] // side
+        label_rows = tiles.shape[0] % side
+        if label_rows:
+            row = tiles[tiles.shape[0] - label_rows :, :].astype(jnp.float32)
+            for slot in range(slots):
+                codes[place_in_list + slot] = row[0, slot].astype(jnp.int32)
+            place_in_list, slots = place_in_list + slots, 0
     for a in range(cols):
         for z in range(halves):
             part = slice(z * vecs, (z + 1) * vecs)
             base_ref[0, a, part, :] = first_ref[a * halves + z, :vecs, :]
             base_ref[1, a, part, :] = first_ref[a * halves + z, vecs:, :]
-    mirror_products(codes, me[0], base_ref.at[0], (t0, t1, t2, t3), send_ref)
-
-
-def second_kernel(codes, me, base_ref, got_ref, t0, t1, t2, t3, send_ref, x_ref):
+    mirror_products(codes, me[0], base_ref.at[0], tile_refs, send_ref)
+
+
+def second_kernel(codes, me, base_ref, got_ref, *refs):
+    *tile_refs, send_ref, x_ref = refs
     for a in range(x_ref.shape[0]):
         x = base_ref[0, a]
         image = base_ref[1, a] * x + summed(got_ref, a)
         x_ref[a] = (image - centre * x) * (sigma_first / half)
-    mirror_products(codes, me[0], x_ref, (t0, t1, t2, t3), send_ref)
-
-
-def third_kernel(codes, me, base_ref, last_ref, got_ref, t0, t1, t2, t3, send_ref, x_ref):
+    mirror_products(codes, me[0], x_ref, tile_refs, send_ref)
+
+
+def third_kernel(codes, me, base_ref, last_ref, got_ref, *refs):
+    *tile_refs, send_ref, x_ref = refs
     for a in range(x_ref.shape[0]):
         x = last_ref[a]
         image = base_ref[1, a] * x + summed(got_ref, a)
         x_ref[a] = (image - centre * x) * (2.0 * sigma_next / half) - (
             sigma_first * sigma_next
         ) * base_ref[0, a]
-    mirror_products(codes, me[0], x_ref, (t0, t1, t2, t3), send_ref)
-
-
-def direct_kernel(codes, me, got_ref, t0, t1, t2, t3, send_ref, sums_ref):
-    direct_products(codes, me[0], got_ref, (t0, t1, t2, t3), sums_ref)
+    mirror_products(codes, me[0], x_ref, tile_refs, send_ref)
+
+
+def direct_kernel(codes, me, got_ref, *refs):
+    *tile_refs, send_ref, sums_ref = refs
+    direct_products(codes, me[0], got_ref, tile_refs, sums_ref)
     for peer in range(send_ref.shape[0]):
         send_ref[peer] = sums_ref[...]
 
 
-def last_direct_kernel(codes, me, base_ref, x_ref, got_ref, t0, t1, t2, t3, send_ref, sums_ref):
-    direct_products(codes, me[0], got_ref, (t0, t1, t2, t3), sums_ref)
+def last_direct_kernel(codes, me, base_ref, x_ref, got_ref, *refs):
+    *tile_refs, send_ref, sums_ref = refs
+    direct_products(codes, me[0], got_ref, tile_refs, sums_ref)
     cols, vecs = sums_ref.shape[0], send_ref.shape[1] // 3
     halves = send_ref.shape[0] // cols
     x = x_ref[me[0]]
@@ -178,14 +197,6 @@
             send_ref[c * halves + z, 2 * vecs :, :] = square
 
 
-def own_part(ref, index, half_index, vecs):
-    block = ref[index]
-    part = block[:vecs]
-    for z in range(1, block.shape[0] // vecs):
-        part = jnp.where(half_index == z, block[z * vecs : (z + 1) * vecs], part)
-    return part
-
-
 def image_kernel(got_ref, image_ref, send_ref):
     vecs = image_ref.shape[0]
     total = got_ref[0]
@@ -203,8 +214,8 @@
         total = total + got_ref[k]
     total = jnp.sum(total, axis=1, keepdims=True)
     ritz = total[:vecs] / (total[vecs:] + 1e-06)
-    x = own_part(x_ref, me[0], me[1], vecs)
-    energy = base_ref[1, me[0]][:vecs]
+    x = x_ref[me[0]]
+    energy = base_ref[1, me[0]]
     resid = energy * x + image_ref[...] - ritz * x
     spacing = energy - ritz
     out_ref[...] = x - spacing / jnp.maximum(spacing * spacing, 1.0) * resid
@@ -222,23 +233,31 @@
     slots, side = tiles.shape[0], tiles.shape[1]
     vecs = vectors.shape[0]
     wide = vecs * halves
-    first, stored, me = pl.pallas_call(
+    early = slots // 2 + 1
+    part_rows = (early * side, (slots - early) * side + LABEL_ROWS)
+    first, *stored, me = pl.pallas_call(
         prepare_kernel,
         out_shape=[
             jax.ShapeDtypeStruct((cols * halves, 2 * vecs, side), jnp.float32),
-            pltpu.VMEM((slots + 1, side, side), tiles.dtype),
-            pltpu.SMEM((2,), jnp.int32),
+            *(pltpu.VMEM((part, side), tiles.dtype) for part in part_rows),
+            pltpu.SMEM((1,), jnp.int32),
         ],
         in_specs=[SMEM] + [VMEM] * 3,
-        out_specs=[VMEM, VMEM, SMEM],
+        out_specs=[VMEM] * (1 + len(part_rows)) + [SMEM],
     )(tile_codes, vectors, energies[None], tiles)
+    swap = [(0, 1), (1, 0)]
+    far = []
+    for part in stored:
+        far.append(lax.ppermute(part, "z_hi", swap))
     first = exchange(first, COL)
-    swap = [(0, 1), (1, 0)]
-    far = lax.ppermute(stored, "z_hi", swap)
-    near = lax.ppermute(stored, "core", swap)
-    far, _ = lax.optimization_barrier((far, first))
-    far_near = lax.ppermute(far, "core", swap)
-    pair = (stored, near, far, far_near)
+    near = []
+    for part in stored:
+        near.append(lax.ppermute(part, "core", swap))
+    far_near = []
+    for part in far:
+        part, _ = lax.optimization_barrier((part, first))
+        far_near.append(lax.ppermute(part, "core", swap))
+    pair = (*stored, *near, *far, *far_near)
 
     row_shape = (rows, 2 * wide, side)
     state_shape = (cols, wide, side)
@@ -248,7 +267,7 @@
         out_shape=[
             pltpu.VMEM(row_shape, jnp.float32),
             pltpu.VMEM((2, *state_shape), jnp.float32),
-            pltpu.SMEM((len(pair) * slots,), jnp.int32),
+            pltpu.SMEM((4 * slots,), jnp.int32),
         ],
         in_specs=[SMEM] + [VMEM] * (1 + len(pair)),
         out_specs=[VMEM, VMEM, SMEM],

time: 160 us -> 158 us (0.988)
  blocking collectives: 117 us -> 109 us
  starting transfers between devices: 26.1 us -> 32.3 us
    all_to_all x7, blocking collectives: 117 us -> 109 us  [exchange(): return lax.all_to_all(blocks, axis, 0, 0, tiled=True)]
    ppermute x3 -> x6, starting transfers between devices: 18.9 us -> 25.2 us  [the longest x2 17 us: on_device(): far.append(lax.ppermute(part, 'z_hi', swap))]
  transfers between devices with their start and end apart: 4 -> 7, of which waited for: 2 -> 2; matrix products, arithmetic and copies ran while one was open for 0% -> 0% of each run, Pallas kernels for 0% -> 0%
where the time goes in v8:
time: 158 us; the launch traced here: 157 us
  blocking collectives  109 us (69%)
  starting transfers between devices  32.3 us (20%)
  Pallas kernels  8.21 us (5%)
  waiting for transfers between devices  7.31 us (5%)
    all_to_all x7, blocking collectives, exchange(): return lax.all_to_all(blocks, axis, 0, 0, tiled=True)  109 us
    ppermute x2, starting transfers between devices, on_device(): far.append(lax.ppermute(part, 'z_hi', swap))  17 us
    all_to_all x1, starting transfers between devices, exchange(): return lax.all_to_all(blocks, axis, 0, 0, tiled=True)  7.11 us
    all_to_all x1, waiting for transfers between devices, exchange(): return lax.all_to_all(blocks, axis, 0, 0, tiled=True)  5.86 us
    pallas_call x7, Pallas kernels, call(): pl.pallas_call(body, out_shape=[space(shape, jnp.float32) for shape in ou...  5.64 us
    ppermute x2, starting transfers between devices, on_device(): near.append(lax.ppermute(part, 'core', swap))  4.31 us
    ppermute x2, starting transfers between devices, on_device(): far_near.append(lax.ppermute(part, 'core', swap))  3.83 us
  transfers between devices with their start and end apart: 7, of which 2 were waited for; matrix products, arithmetic and copies ran while one was open for 0% of the time, Pallas kernels for 0%

profile of v8, /device:TPU:2, one launch (start us, length us, event | category | flops | bytes accessed | tf_op | source)
XLA Modules:
  0.0 157.3 jit_solution(12108545461453657211)
XLA Ops:
  0.6 1.7 %shard_map.59 = (f32[8,4,128]{2,1,0:T(4,128)}, bf16[1024,128]{1,0:T(8,128)(2,1)S(1)}, bf16[912,128]{1,0:T(8,128)(2,1)S(1)}, s32[1]{0:T(128)S(4)}) custom-call(s32[15]{0:T(128)} %codes.1, f32[2,128]{1,0:T(2,128)} %vectors_ref.1, f32[1,128]{1,0:T(1,128)} %bitcast.2, bf16[15,128,128]{2,1,0:T(8,128)(2,1)} %tiles_ref.1), custom_call_target="tpu_custom_call" | custom-call | tf_op jit(solution)/shard_map/pallas_call | solution.py:238
  2.3 15.1 %collective-permute-start.2 = (bf16[1024,128]{1,0:T(8,128)(2,1)S(1)}, bf16[1024,128]{1,0:T(8,128)(2,1)S(1)}, u32[]{:S(2)}, u32[]{:S(2)}) collective-permute-start(bf16[1024,128]{1,0:T(8,128)(2,1)S(1)} %get-tuple-element.21.refs_0_), channel_id=1, source_target_pairs={{0,2},{2,0},{1,3},{3,1},{4,6},{6,4},{5,7},{7,5},{8,10},{10,8},{9,1... | collective-permute-start | bytes 786440 | tf_op jit(solution)/shard_map/ppermute | solution.py:251
  17.5 1.9 %collective-permute-start.3 = (bf16[912,128]{1,0:T(8,128)(2,1)S(1)}, bf16[912,128]{1,0:T(8,128)(2,1)S(1)}, u32[]{:S(2)}, u32[]{:S(2)}) collective-permute-start(bf16[912,128]{1,0:T(8,128)(2,1)S(1)} %get-tuple-element.22.refs_1_), channel_id=1, source_target_pairs={{0,2},{2,0},{1,3},{3,1},{4,6},{6,4},{5,7},{7,5},{8,10},{10,8},{9,1... | collective-permute-start | bytes 700424 | tf_op jit(solution)/shard_map/ppermute | solution.py:251
  19.4 7.1 %all-to-all-start = ((f32[8,4,128]{2,1,0:T(4,128)}), f32[8,4,128]{2,1,0:T(4,128)S(1)}, u32[]{:S(2)}, u32[]{:S(2)}) async-start(f32[8,4,128]{2,1,0:T(4,128)} %get-tuple-element.20), calls=%async_computation | async-start | bytes 32768 | tf_op jit(solution)/shard_map/all_to_all | solution.py:31
  26.5 1.9 %collective-permute-start = (bf16[1024,128]{1,0:T(8,128)(2,1)S(1)}, bf16[1024,128]{1,0:T(8,128)(2,1)S(1)}, u32[]{:S(2)}, u32[]{:S(2)}) collective-permute-start(bf16[1024,128]{1,0:T(8,128)(2,1)S(1)} %get-tuple-element.21.refs_0_), channel_id=1, source_target_pairs={{0,1},{1,0},{2,3},{3,2},{4,5},{5,4},{6,7},{7,6},{8,9},{9,8},{10,11... | collective-permute-start | bytes 786440 | tf_op jit(solution)/shard_map/ppermute | solution.py:255
  28.4 5.9 %all-to-all-done.first_ref = f32[8,4,128]{2,1,0:T(4,128)S(1)} async-done(((f32[8,4,128]{2,1,0:T(4,128)}), f32[8,4,128]{2,1,0:T(4,128)S(1)}, u32[]{:S(2)}, u32[]{:S(2)}) %all-to-all-start) | async-done | bytes 16416 | tf_op jit(solution)/shard_map/all_to_all | solution.py:31
  34.3 0.0 collective-permute-done.2.refs_4_
  34.3 1.9 %collective-permute-start.4 = (bf16[1024,128]{1,0:T(8,128)(2,1)S(1)}, bf16[1024,128]{1,0:T(8,128)(2,1)S(1)}, u32[]{:S(2)}, u32[]{:S(2)}) collective-permute-start(bf16[1024,128]{1,0:T(8,128)(2,1)S(1)} %collective-permute-done.2.refs_4_), channel_id=1, source_target_pairs={{0,1},{1,0},{2,3},{3,2},{4,5},{5,4},{6,7},{7,6},{8,9},{9,8},{10,11... | collective-permute-start | bytes 786440 | tf_op jit(solution)/shard_map/ppermute | solution.py:259
  36.2 2.4 %collective-permute-start.1 = (bf16[912,128]{1,0:T(8,128)(2,1)S(1)}, bf16[912,128]{1,0:T(8,128)(2,1)S(1)}, u32[]{:S(2)}, u32[]{:S(2)}) collective-permute-start(bf16[912,128]{1,0:T(8,128)(2,1)S(1)} %get-tuple-element.22.refs_1_), channel_id=1, source_target_pairs={{0,1},{1,0},{2,3},{3,2},{4,5},{5,4},{6,7},{7,6},{8,9},{9,8},{10,11... | collective-permute-start | bytes 700424 | tf_op jit(solution)/shard_map/ppermute | solution.py:255
  38.6 0.0 collective-permute-done.3.refs_5_
  38.6 1.9 %collective-permute-start.5 = (bf16[912,128]{1,0:T(8,128)(2,1)S(1)}, bf16[912,128]{1,0:T(8,128)(2,1)S(1)}, u32[]{:S(2)}, u32[]{:S(2)}) collective-permute-start(bf16[912,128]{1,0:T(8,128)(2,1)S(1)} %collective-permute-done.3.refs_5_), channel_id=1, source_target_pairs={{0,1},{1,0},{2,3},{3,2},{4,5},{5,4},{6,7},{7,6},{8,9},{9,8},{10,11... | collective-permute-start | bytes 700424 | tf_op jit(solution)/shard_map/ppermute | solution.py:259
  40.6 0.0 collective-permute-done.1.refs_3_
  40.6 0.0 collective-permute-done.refs_2_
  40.6 1.4 collective-permute-done.5.refs_7_
  42.0 0.0 collective-permute-done.4.refs_6_
  42.0 0.9 shard_map.60
  42.9 30.1 %all_to_all.40.got_ref = f32[24,4,128]{2,1,0:T(4,128)S(1)} all-to-all(f32[24,4,128]{2,1,0:T(4,128)S(1)} %get-tuple-element.27), channel_id=1, replica_groups=mesh['z_lo'=6,'x'=4,'col'=8,'z_hi'=2,'core'=2] {'z_lo','x'}, dimensions={0} | all-to-all | bytes 98304 | tf_op jit(solution)/shard_map/all_to_all | solution.py:31
  73.0 1.2 shard_map.61
  74.2 15.3 %all_to_all.41.got_ref = f32[8,8,2,128]{3,2,1,0:T(2,128)S(1)} all-to-all(f32[8,8,2,128]{3,2,1,0:T(2,128)S(1)} %shard_map.61), channel_id=1, replica_groups=mesh['z_lo'=6,'x'=4,'col'=8,'z_hi'=2,'core'=2] {'col'}, dimensions={0} | all-to-all | bytes 131072 | tf_op jit(solution)/shard_map/all_to_all | solution.py:31
  89.5 0.7 shard_map.62
  90.2 14.1 %all_to_all.42.got_ref = f32[24,4,128]{2,1,0:T(4,128)S(1)} all-to-all(f32[24,4,128]{2,1,0:T(4,128)S(1)} %get-tuple-element.29), channel_id=1, replica_groups=mesh['z_lo'=6,'x'=4,'col'=8,'z_hi'=2,'core'=2] {'z_lo','x'}, dimensions={0} | all-to-all | bytes 98304 | tf_op jit(solution)/shard_map/all_to_all | solution.py:31
  104.2 1.2 shard_map.63
  105.4 10.8 %all_to_all.43.got_ref = f32[8,8,2,128]{3,2,1,0:T(2,128)S(1)} all-to-all(f32[8,8,2,128]{3,2,1,0:T(2,128)S(1)} %shard_map.63), channel_id=1, replica_groups=mesh['z_lo'=6,'x'=4,'col'=8,'z_hi'=2,'core'=2] {'col'}, dimensions={0} | all-to-all | bytes 131072 | tf_op jit(solution)/shard_map/all_to_all | solution.py:31
  116.2 0.7 shard_map.64
  116.8 14.1 %all_to_all.44.got_ref = f32[24,4,128]{2,1,0:T(4,128)S(1)} all-to-all(f32[24,4,128]{2,1,0:T(4,128)S(1)} %get-tuple-element.31), channel_id=1, replica_groups=mesh['z_lo'=6,'x'=4,'col'=8,'z_hi'=2,'core'=2] {'z_lo','x'}, dimensions={0} | all-to-all | bytes 98304 | tf_op jit(solution)/shard_map/all_to_all | solution.py:31
  130.9 1.2 shard_map.65
  132.1 10.4 %all_to_all.45.got_ref = f32[8,6,128]{2,1,0:T(8,128)S(1)} all-to-all(f32[8,6,128]{2,1,0:T(8,128)S(1)} %shard_map.65), channel_id=1, replica_groups=mesh['z_lo'=6,'x'=4,'col'=8,'z_hi'=2,'core'=2] {'col'}, dimensions={0} | all-to-all | bytes 49152 | tf_op jit(solution)/shard_map/all_to_all | solution.py:31
  142.5 14.0 %all_to_all.46.got_ref = f32[24,4,128]{2,1,0:T(4,128)S(1)} all-to-all(f32[24,4,128]{2,1,0:T(4,128)S(1)} %get-tuple-element.33), channel_id=1, replica_groups=mesh['z_lo'=6,'x'=4,'col'=8,'z_hi'=2,'core'=2] {'z_lo','x'}, dimensions={0} | all-to-all | bytes 98304 | tf_op jit(solution)/shard_map/all_to_all | solution.py:31
  156.5 0.8 shard_map.67
  (1 shorter events, 0.0 us)
Async XLA Ops:
  2.3 32.0 %collective-permute-start.2 = (bf16[1024,128]{1,0:T(8,128)(2,1)S(1)}, bf16[1024,128]{1,0:T(8,128)(2,1)S(1)}, u32[]{:S(2)}, u32[]{:S(2)}) collective-permute-start(bf16[1024,128]{1,0:T(8,128)(2,1)S(1)} %get-tuple-element.21.refs_0_), channel_id=1, source_target_pairs={{0,2},{2,0},{1,3},{3,1},{4,6},{6,4},{5,7},{7,5},{8,10},{10,8},{9,1... | collective-permute-start | bytes 786440 | tf_op jit(solution)/shard_map/ppermute | solution.py:251
  17.5 21.2 %collective-permute-start.3 = (bf16[912,128]{1,0:T(8,128)(2,1)S(1)}, bf16[912,128]{1,0:T(8,128)(2,1)S(1)}, u32[]{:S(2)}, u32[]{:S(2)}) collective-permute-start(bf16[912,128]{1,0:T(8,128)(2,1)S(1)} %get-tuple-element.22.refs_1_), channel_id=1, source_target_pairs={{0,2},{2,0},{1,3},{3,1},{4,6},{6,4},{5,7},{7,5},{8,10},{10,8},{9,1... | collective-permute-start | bytes 700424 | tf_op jit(solution)/shard_map/ppermute | solution.py:251
  19.4 14.9 %all-to-all-start = ((f32[8,4,128]{2,1,0:T(4,128)}), f32[8,4,128]{2,1,0:T(4,128)S(1)}, u32[]{:S(2)}, u32[]{:S(2)}) async-start(f32[8,4,128]{2,1,0:T(4,128)} %get-tuple-element.20), calls=%async_computation | async-start | bytes 32768 | tf_op jit(solution)/shard_map/all_to_all | solution.py:31
  26.5 14.1 %collective-permute-start = (bf16[1024,128]{1,0:T(8,128)(2,1)S(1)}, bf16[1024,128]{1,0:T(8,128)(2,1)S(1)}, u32[]{:S(2)}, u32[]{:S(2)}) collective-permute-start(bf16[1024,128]{1,0:T(8,128)(2,1)S(1)} %get-tuple-element.21.refs_0_), channel_id=1, source_target_pairs={{0,1},{1,0},{2,3},{3,2},{4,5},{5,4},{6,7},{7,6},{8,9},{9,8},{10,11... | collective-permute-start | bytes 786440 | tf_op jit(solution)/shard_map/ppermute | solution.py:255
  34.3 7.7 %collective-permute-start.4 = (bf16[1024,128]{1,0:T(8,128)(2,1)S(1)}, bf16[1024,128]{1,0:T(8,128)(2,1)S(1)}, u32[]{:S(2)}, u32[]{:S(2)}) collective-permute-start(bf16[1024,128]{1,0:T(8,128)(2,1)S(1)} %collective-permute-done.2.refs_4_), channel_id=1, source_target_pairs={{0,1},{1,0},{2,3},{3,2},{4,5},{5,4},{6,7},{7,6},{8,9},{9,8},{10,11... | collective-permute-start | bytes 786440 | tf_op jit(solution)/shard_map/ppermute | solution.py:259
  36.2 4.4 %collective-permute-start.1 = (bf16[912,128]{1,0:T(8,128)(2,1)S(1)}, bf16[912,128]{1,0:T(8,128)(2,1)S(1)}, u32[]{:S(2)}, u32[]{:S(2)}) collective-permute-start(bf16[912,128]{1,0:T(8,128)(2,1)S(1)} %get-tuple-element.22.refs_1_), channel_id=1, source_target_pairs={{0,1},{1,0},{2,3},{3,2},{4,5},{5,4},{6,7},{7,6},{8,9},{9,8},{10,11... | collective-permute-start | bytes 700424 | tf_op jit(solution)/shard_map/ppermute | solution.py:255
  38.6 3.4 %collective-permute-start.5 = (bf16[912,128]{1,0:T(8,128)(2,1)S(1)}, bf16[912,128]{1,0:T(8,128)(2,1)S(1)}, u32[]{:S(2)}, u32[]{:S(2)}) collective-permute-start(bf16[912,128]{1,0:T(8,128)(2,1)S(1)} %collective-permute-done.3.refs_5_), channel_id=1, source_target_pairs={{0,1},{1,0},{2,3},{3,2},{4,5},{5,4},{6,7},{7,6},{8,9},{9,8},{10,11... | collective-permute-start | bytes 700424 | tf_op jit(solution)/shard_map/ppermute | solution.py:259
